TPU v7x, 32 devices: a whole 2x2x4 slice. The times are simulated.
32 devices in a mesh: ep: 16 (over z, x, core), vp: 2 (over y).
Axes of the slice: x: 2, y: 2, z: 4, core: 2. Of those that a mesh axis runs over, the one named last changes fastest.
Arguments:
- prefill_tokens: bfloat16 [1024, 2048], P('ep'), may hold values from -6 to 6
- decode_tokens: bfloat16 [64, 2048], P('ep'), may hold values from -6 to 6
- request_order: int32 [64], replicated, may hold values from 0 to 63, each once
- prefill_lengths: int32 [16], P('ep'), may hold values from 1 to 256, 2048 in all
- decode_lengths: int32 [64], P('ep'), may hold values from 1 to 256, 8192 in all
- latent_cache: bfloat16 [80, 256, 576], P('ep'), may hold values from -6 to 6
- attn_gain: float32 [2048], replicated, may hold values from 0.1 to 1.9
- w_query: bfloat16 [2048, 1536], P(None, 'vp'), may hold values from -0.125 to 0.125
- w_latent: bfloat16 [2048, 576], replicated, may hold values from -0.125 to 0.125
- latent_gain: float32 [512], replicated, may hold values from 0.1 to 1.9
- key_up: bfloat16 [512, 1024], P(None, 'vp'), may hold values from -0.5 to 0.5
- value_up: bfloat16 [512, 1024], P(None, 'vp'), may hold values from -0.25 to 0.25
- w_out: bfloat16 [1024, 2048], P('vp'), may hold values from -0.1875 to 0.1875
- ffn_gain: float32 [2048], replicated, may hold values from 0.1 to 1.9
- expert_ids: int32 [1088, 6], P('ep'), may hold values from 0 to 15, all different within a row; in each aligned block of 68 rows (0 to 67, 68 to 135, ...) at most 51 rows name the same one
- expert_weights: float32 [1088, 6], P('ep'), may hold values from 0.05 to 0.45
- w_gate: bfloat16 [16, 2048, 1408], P('ep', None, 'vp'), may hold values from -0.125 to 0.125
- w_up: bfloat16 [16, 2048, 1408], P('ep', None, 'vp'), may hold values from -0.125 to 0.125
- w_down: bfloat16 [16, 1408, 2048], P('ep', 'vp'), may hold values from -0.15625 to 0.15625
- final_gain: float32 [2048], replicated, may hold values from 0.1 to 1.9
- head_weight: bfloat16 [2048, 51200], P(None, ('ep', 'vp')), may hold values from -0.375 to 0.375
Outputs:
- layer_out: bfloat16 [1088, 2048], P('ep', 'vp')
- logits: float32 [80, 51200], P(None, ('ep', 'vp'))
Inputs may be any that keep to these rules, and one draw needn't show every extreme that they name: `request_order`: each decode request appears in exactly one batch slot. `prefill_lengths`: some prefill request has 256 cached positions. `decode_lengths`: some decode request has 256 cached positions. `expert_ids`: each row names 6 different experts. Among the rows of one owner no expert is named more than 51 times, and in some owner's rows one expert is named exactly 51 times.
All inputs are finite; a program needn't handle non-finite values. No bound on the sum of `prefill_lengths` or of `decode_lengths` on one device may be relied on, other than what follows from the above.
Results may differ from a plain program's by a relative error of at most 0.0086.
Values may be sent and summed in bfloat16 or wider, within the bound.
A program may use at most 128 MiB of HBM per device.

v0:
```python
import jax
import jax.numpy as jnp
from jax import lax
from jax.sharding import PartitionSpec as P

NOPE = 128
ROPE = 64
VD = 128
LAT = 512
TOPK = 6


epsilon = 1e-06
rope_base = 10000.0


def rms_norm(values, gain):
    return values * lax.rsqrt(jnp.mean(values * values, axis=-1, keepdims=True) + epsilon) * gain


def rotate(values, positions):
    half_width = values.shape[-1] // 2
    frequency = rope_base ** (-jnp.arange(half_width, dtype=jnp.float32) * 2.0 / values.shape[-1])
    angles = positions.astype(jnp.float32)[..., None] * frequency
    cosines = jnp.cos(angles)
    sines = jnp.sin(angles)
    lower_half = values[..., :half_width]
    upper_half = values[..., half_width:]
    return jnp.concatenate(
        [lower_half * cosines - upper_half * sines, lower_half * sines + upper_half * cosines],
        axis=-1,
    )


def attend(
    prefill_rows,
    decode_rows,
    cached,
    prefill_len,
    decode_len,
    attn_gain,
    w_query,
    w_latent,
    latent_gain,
    key_up,
    value_up,
    w_out,
):
    tokens = jnp.concatenate([prefill_rows, decode_rows], axis=0)
    prefill_count = prefill_rows.shape[0]
    row_count = tokens.shape[0]
    head_count = w_query.shape[1] // (NOPE + ROPE)
    positions = jnp.concatenate(
        [prefill_len[0] + jnp.arange(prefill_count, dtype=jnp.int32), decode_len]
    )
    normed = rms_norm(tokens.astype(jnp.float32), attn_gain).astype(jnp.bfloat16)
    queries = jnp.dot(normed, w_query, preferred_element_type=jnp.float32).reshape(
        row_count, head_count, NOPE + ROPE
    )
    query_nope = queries[..., :NOPE].astype(jnp.bfloat16)
    query_rope = rotate(queries[..., NOPE:], positions[:, None]).astype(jnp.bfloat16)
    latent = jnp.dot(normed, w_latent, preferred_element_type=jnp.float32)
    latent_normed = rms_norm(latent[:, :LAT], latent_gain)
    new_keys = jnp.concatenate([latent_normed, rotate(latent[:, LAT:], positions)], axis=1).astype(
        jnp.bfloat16
    )
    key_heads = key_up.reshape(LAT, head_count, NOPE)
    absorbed = jnp.einsum(
        "rhn,lhn->rhl", query_nope, key_heads, preferred_element_type=jnp.float32
    ).astype(jnp.bfloat16)
    query_all = jnp.concatenate([absorbed, query_rope], axis=-1)
    factor = 1.0 / jnp.sqrt(jnp.float32(NOPE + ROPE))
    cache_len = cached.shape[1]
    prefill_keys = jnp.concatenate([cached[0], new_keys[:prefill_count]], axis=0)
    scores = (
        jnp.einsum(
            "chk,jk->chj",
            query_all[:prefill_count],
            prefill_keys,
            preferred_element_type=jnp.float32,
        )
        * factor
    )
    key_index = jnp.arange(cache_len + prefill_count, dtype=jnp.int32)
    row_index = jnp.arange(prefill_count, dtype=jnp.int32)
    visible = jnp.where(
        key_index[None, :] < cache_len,
        key_index[None, :] < prefill_len[0],
        key_index[None, :] - cache_len <= row_index[:, None],
    )
    expo = jnp.exp(jnp.where(visible[:, None, :], scores, -jnp.inf))
    attn_probs = (expo / jnp.sum(expo, axis=-1, keepdims=True)).astype(jnp.bfloat16)
    prefill_context = jnp.einsum(
        "chj,jl->chl", attn_probs, prefill_keys[:, :LAT], preferred_element_type=jnp.float32
    ).astype(jnp.bfloat16)
    decode_query = query_all[prefill_count:]
    decode_cache = cached[1:]
    own_keys = new_keys[prefill_count:]
    cache_scores = (
        jnp.einsum("dhk,dsk->dhs", decode_query, decode_cache, preferred_element_type=jnp.float32)
        * factor
    )
    self_scores = (
        jnp.einsum("dhk,dk->dh", decode_query, own_keys, preferred_element_type=jnp.float32)
        * factor
    )
    cache_visible = jnp.arange(cache_len, dtype=jnp.int32)[None, :] < decode_len[:, None]
    cache_expo = jnp.exp(jnp.where(cache_visible[:, None, :], cache_scores, -jnp.inf))
    self_expo = jnp.exp(self_scores)
    totals = jnp.sum(cache_expo, axis=-1) + self_expo
    cache_probs = (cache_expo / totals[..., None]).astype(jnp.bfloat16)
    self_probs = (self_expo / totals).astype(jnp.bfloat16)
    decode_context = jnp.einsum(
        "dhs,dsl->dhl", cache_probs, decode_cache[..., :LAT], preferred_element_type=jnp.float32
    )
    decode_context = (
        decode_context
        + self_probs.astype(jnp.float32)[..., None] * own_keys[:, None, :LAT].astype(jnp.float32)
    ).astype(jnp.bfloat16)
    context = jnp.concatenate([prefill_context, decode_context], axis=0)
    value_heads = value_up.reshape(LAT, head_count, VD)
    head_out = jnp.einsum(
        "rhl,lhv->rhv", context, value_heads, preferred_element_type=jnp.float32
    ).astype(jnp.bfloat16)
    return jnp.dot(
        head_out.reshape(row_count, head_count * VD), w_out, preferred_element_type=jnp.float32
    )


def on_device(
    prefill_tokens,
    decode_tokens,
    request_order,
    prefill_lengths,
    decode_lengths,
    latent_cache,
    attn_gain,
    w_query,
    w_latent,
    latent_gain,
    key_up,
    value_up,
    w_out,
    ffn_gain,
    expert_ids,
    expert_weights,
    w_gate,
    w_up,
    w_down,
    final_gain,
    head_weight,
):
    owners = lax.axis_size("ep")
    shards = lax.axis_size("vp")
    partial_attn = attend(
        prefill_tokens,
        decode_tokens,
        latent_cache,
        prefill_lengths,
        decode_lengths,
        attn_gain,
        w_query,
        w_latent,
        latent_gain,
        key_up,
        value_up,
        w_out,
    )
    attn = lax.psum(partial_attn, "vp")
    tokens = jnp.concatenate([prefill_tokens, decode_tokens], axis=0)
    resid = (tokens.astype(jnp.float32) + attn).astype(jnp.bfloat16)
    ffn_in = rms_norm(resid.astype(jnp.float32), ffn_gain).astype(jnp.bfloat16)
    row_count = tokens.shape[0]
    model_width = tokens.shape[1]
    share_width = model_width // shards
    capacity = max(2, min(row_count, row_count * TOPK * 2 // owners))
    flat_ids = expert_ids.reshape(-1)
    onehot = (flat_ids[:, None] == jnp.arange(owners, dtype=jnp.int32)[None, :]).astype(jnp.int32)
    earlier = jnp.cumsum(onehot, axis=0) - onehot
    slot_index = jnp.sum(earlier * onehot, axis=1)
    target = flat_ids * capacity + slot_index
    source_rows = jnp.arange(row_count * TOPK, dtype=jnp.int32) // TOPK
    outgoing = (
        jnp.zeros((owners * capacity, model_width), jnp.bfloat16)
        .at[target]
        .set(ffn_in[source_rows])
    )
    outgoing = outgoing.reshape(owners, capacity, model_width)
    arrived = lax.all_to_all(outgoing, "ep", split_axis=0, concat_axis=0, tiled=True)
    item_count = arrived.shape[1]
    flattened = arrived.reshape(owners * item_count, model_width)
    gated = jnp.dot(flattened, w_gate[0], preferred_element_type=jnp.float32)
    upward = jnp.dot(flattened, w_up[0], preferred_element_type=jnp.float32)
    hidden_act = (jax.nn.silu(gated) * upward).astype(jnp.bfloat16)
    result = jnp.dot(hidden_act, w_down[0], preferred_element_type=jnp.float32).reshape(
        owners, item_count, model_width
    )
    summed = lax.psum_scatter(result, "vp", scatter_dimension=2, tiled=True)
    sent_back = lax.all_to_all(summed, "ep", split_axis=0, concat_axis=0, tiled=True)
    picked = sent_back.reshape(owners * capacity, sent_back.shape[2])[target]
    picked = picked.reshape(row_count, TOPK, sent_back.shape[2])
    routed_sum = jnp.sum(expert_weights[:, :, None] * picked, axis=1)
    column = lax.axis_index("vp") * share_width
    resid_share = lax.dynamic_slice_in_dim(resid, column, share_width, 1)
    layer_out = (resid_share.astype(jnp.float32) + routed_sum).astype(jnp.bfloat16)
    prefill_count = prefill_tokens.shape[0]
    decode_count = decode_tokens.shape[0]
    own_rows = layer_out[prefill_count - 1 :]
    everyone = lax.all_gather(own_rows, ("ep", "vp"), axis=0, tiled=True)
    everyone = everyone.reshape(owners, shards, 1 + decode_count, share_width)
    everyone = jnp.transpose(everyone, (0, 2, 1, 3)).reshape(owners, 1 + decode_count, model_width)
    prefill_last = everyone[:, 0]
    decode_rows = everyone[:, 1:].reshape(owners * decode_count, model_width)[request_order]
    final_rows = jnp.concatenate([prefill_last, decode_rows], axis=0)
    final_normed = rms_norm(final_rows.astype(jnp.float32), final_gain).astype(jnp.bfloat16)
    logits = jnp.dot(final_normed, head_weight, preferred_element_type=jnp.float32)
    return (layer_out, logits)


def solution(mesh):
    return jax.shard_map(
        on_device,
        mesh=mesh,
        in_specs=(
            P("ep", None),
            P("ep", None),
            P(),
            P("ep"),
            P("ep"),
            P("ep", None, None),
            P(),
            P(None, "vp"),
            P(),
            P(),
            P(None, "vp"),
            P(None, "vp"),
            P("vp", None),
            P(),
            P("ep", None),
            P("ep", None),
            P("ep", None, "vp"),
            P("ep", None, "vp"),
            P("ep", "vp", None),
            P(),
            P(None, ("ep", "vp")),
        ),
        out_specs=(P("ep", "vp"), P(None, ("ep", "vp"))),
        check_vma=False,
    )
```

profile of v0, /device:TPU:0, one launch (start us, length us, event | category | flops | bytes accessed | tf_op | source)
XLA Modules:
  0.0 450.3 jit_solution(14517979660275451987)
XLA Ops:
  10.7 3.3 fusion.84
  14.0 1.4 fusion.86
  19.1 1.5 fusion.15
  23.1 1.6 convolution_convert_fusion.1
  24.7 1.6 fusion.26
  26.5 1.3 fusion.16
  27.9 1.3 fusion.90
  31.5 30.6 %all-reduce.3.cloned.1.call-done = f32[68,2048]{1,0:T(8,128)} async-done(((f32[68,2048]{1,0:T(8,128)}), f32[68,2048]{1,0:T(8,128)}) %all-reduce.3.cloned.1.call-update) | async-done | bytes 557072 | tf_op jit(solution)/shard_map/psum | solution.py:169
  64.3 10.3 %scatter_custom_fusion = bf16[816,2048]{1,0:T(8,128)(2,1)S(1)} fusion(s32[408]{0:T(512)S(1)} %bitcast.89, bf16[68,2048]{1,0:T(8,128)(2,1)} %fusion.33, s32[1024]{0:T(1024)S(1)} %pad_clamp_fusion.2, bf16[]{:T(256)} %constant.63.clone.1), kind=kCustom, calls=%fused_computation.12 | custom fusion | bytes 3342848 | tf_op jit(solution)/shard_map/scatter | solution.py:186
  74.6 2.3 reshape.346
  76.9 86.7 %all_to_all.10 = bf16[16,51,2048]{2,1,0:T(8,128)(2,1)} all-to-all(bf16[16,51,2048]{2,1,0:T(8,128)(2,1)} %reshape.346), channel_id=1, replica_groups=mesh['ep'=16,'vp'=2] {'ep'}, dimensions={0} | all-to-all | bytes 6684672 | tf_op jit(solution)/shard_map/all_to_all | solution.py:189
  163.7 2.6 reshape.347
  166.3 4.7 %fusion.2 = f32[816,704]{1,0:T(8,128)S(1)} fusion(bf16[816,2048]{1,0:T(8,128)(2,1)S(1)} %reshape.347, bf16[1,2048,704]{1,2,0:T(8,128)(2,1)} %param.38), kind=kOutput, calls=%fused_computation.6 | convolution fusion | flops 2353004544 | bytes 8523776 | tf_op jit(solution)/shard_map/dot_general | solution.py:193
  171.1 4.2 multiply_convert_fusion
  175.3 1.5 dot_general.56
  176.8 6.9 %fusion = f32[16,51,2048]{2,1,0:T(8,128)} fusion(bf16[16,51,704]{2,1,0:T(8,128)(2,1)S(1)} %dot_general.56, bf16[1,704,2048]{2,1,0:T(8,128)(2,1)} %param.39), kind=kOutput, calls=%fused_computation.4 | convolution fusion | flops 2353004544 | bytes 10717184 | tf_op jit(solution)/shard_map/dot_general | solution.py:195
  183.7 88.2 %reduce-scatter.2.cloned.1.call-done = f32[16,51,1024]{2,1,0:T(8,128)} async-done(((f32[16,51,2048]{2,1,0:T(8,128)}), f32[16,51,1024]{2,1,0:T(8,128)}) %reduce-scatter.2.cloned.1.call-update) | async-done | bytes 3342352 | tf_op jit(solution)/shard_map/reduce_scatter | solution.py:198
  271.9 5.7 %all-to-all-start.1 = ((f32[16,51,1024]{2,1,0:T(8,128)}), f32[16,51,1024]{2,1,0:T(8,128)}, u32[]{:S(2)}, u32[]{:S(2)}) async-start(f32[16,51,1024]{2,1,0:T(8,128)} %reduce-scatter.2.cloned.1.call-done), calls=%async_computation.2 | async-start | bytes 7340032 | tf_op jit(solution)/shard_map/all_to_all | solution.py:199
  277.7 68.4 %all-to-all-done.1 = f32[16,51,1024]{2,1,0:T(8,128)} async-done(((f32[16,51,1024]{2,1,0:T(8,128)}), f32[16,51,1024]{2,1,0:T(8,128)}, u32[]{:S(2)}, u32[]{:S(2)}) %all-to-all-start.1) | async-done | bytes 3342368 | tf_op jit(solution)/shard_map/all_to_all | solution.py:199
  346.1 2.3 reshape.348
  348.4 2.5 gather_fusion
  350.9 1.5 reshape.349
  353.3 82.4 %all-gather = bf16[32,5,1024]{2,1,0:T(8,128)(2,1)S(1)} all-gather(bf16[1,5,1024]{2,1,0:T(8,128)(2,1)S(1)} %slice_bitcast_fusion.1), channel_id=1, replica_groups=mesh['ep'=16,'vp'=2] {'ep','vp'}, dimensions={0}, use_global_device_ids=true | all-gather | bytes 337920 | tf_op jit(solution)/shard_map/all_gather | solution.py:209
  437.6 5.9 %fusion.48 = f32[80,1600]{1,0:T(8,128)} fusion(bf16[2048,1600]{0,1:T(8,128)(2,1)} %param.41, f32[2048]{0:T(1024)S(1)} %copy-done.13, f32[80]{0:T(128)S(1)} %add_rsqrt_fusion, bf16[64,2048]{1,0:T(8,128)(2,1)S(1)} %gather_fusion.1, bf16[16,2048]{1,0:T(8,128)(2,1)S(1)} %slice_bitcast_fusion), kind=kOutput, calls=%fused_computation.60 | convolution fusion | flops 525434880 | bytes 7401792 | tf_op jit(solution)/shard_map/dot_general | solution.py:216
  (111 shorter events, 16.2 us)
Async XLA Ops:
  7.2 6.9 %copy-start = (bf16[2048,768]{1,0:T(8,128)(2,1)S(1)}, bf16[2048,768]{1,0:T(8,128)(2,1)}, u32[]{:S(2)}) copy-start(bf16[2048,768]{1,0:T(8,128)(2,1)} %param.28) | copy-start | bytes 9437188
  7.2 6.8 %copy-start.2 = (bf16[64,2048]{1,0:T(8,128)(2,1)S(1)}, bf16[64,2048]{1,0:T(8,128)(2,1)}, u32[]{:S(2)}) copy-start(bf16[64,2048]{1,0:T(8,128)(2,1)} %param.21) | copy-start | bytes 786436
  7.2 6.8 %copy-start.8 = (bf16[4,2048]{1,0:T(4,128)(2,1)S(1)}, bf16[4,2048]{1,0:T(4,128)(2,1)}, u32[]{:S(2)}) copy-start(bf16[4,2048]{1,0:T(4,128)(2,1)} %param.22) | copy-start | bytes 49156
  7.2 6.8 %copy-start.10 = (f32[2048]{0:T(1024)S(1)}, f32[2048]{0:T(1024)}, u32[]{:S(2)}) copy-start(f32[2048]{0:T(1024)} %param.27) | copy-start | bytes 24580
  7.2 54.9 %all-reduce.3.cloned.1.call-start = ((), (), s32[]{:S(2)}) async-start(), calls=%async_computation.3 | async-start | bytes 1179648 | tf_op jit(solution)/shard_map/psum | solution.py:169
  15.4 5.4 %copy-start.6 = (f32[68,576]{1,0:T(8,128)S(1)}, f32[68,576]{1,0:T(8,128)}, u32[]{:S(2)}) copy-start(f32[68,576]{1,0:T(8,128)} %fusion.84) | copy-start | bytes 470020
  15.5 5.4 %copy-start.15 = (f32[512]{0:T(512)S(1)}, f32[512]{0:T(512)}, u32[]{:S(2)}) copy-start(f32[512]{0:T(512)} %param.30) | copy-start | bytes 6148
  15.5 5.8 %copy-start.7 = (bf16[5,256,576]{1,2,0:T(8,128)(2,1)S(1)}, bf16[5,256,576]{1,2,0:T(8,128)(2,1)}, u32[]{:S(2)}) copy-start(bf16[5,256,576]{1,2,0:T(8,128)(2,1)} %param.26) | copy-start | bytes 4423684
  19.1 2.7 slice-start
  23.1 4.7 %copy-start.3 = (bf16[512,2048]{1,0:T(8,128)(2,1)S(1)}, bf16[512,2048]{1,0:T(8,128)(2,1)}, u32[]{:S(2)}) copy-start(bf16[512,2048]{1,0:T(8,128)(2,1)} %param.33) | copy-start | bytes 6291460
  26.4 3.0 copy-start.11
  27.8 35.6 %copy-start.12 = (f32[2048]{0:T(1024)S(1)}, f32[2048]{0:T(1024)}, u32[]{:S(2)}) copy-start(f32[2048]{0:T(1024)} %param.34) | copy-start | bytes 24580
  29.2 242.7 %reduce-scatter.2.cloned.1.call-start = ((), (), s32[]{:S(2)}) async-start(), calls=%async_computation.4 | async-start | bytes 11010048 | tf_op jit(solution)/shard_map/reduce_scatter | solution.py:198
  63.4 0.9 copy-start.4
  166.3 4.8 %copy-start.16 = (bf16[1,2048,704]{1,2,0:T(8,128)(2,1)S(1)}, bf16[1,2048,704]{1,2,0:T(8,128)(2,1)}, u32[]{:S(2)}) copy-start(bf16[1,2048,704]{1,2,0:T(8,128)(2,1)} %param.37) | copy-start | bytes 8650756
  183.7 93.9 %copy-start.14 = (f32[68,6]{0,1:T(8,128)S(1)}, f32[68,6]{0,1:T(8,128)}, u32[]{:S(2)}) copy-start(f32[68,6]{0,1:T(8,128)} %param.36) | copy-start | bytes 4900
  183.7 94.0 %copy-start.17 = (s32[64]{0:T(128)S(1)}, s32[64]{0:T(128)}, u32[]{:S(2)}) copy-start(s32[64]{0:T(128)} %param.23) | copy-start | bytes 772
  271.9 74.2 %all-to-all-start.1 = ((f32[16,51,1024]{2,1,0:T(8,128)}), f32[16,51,1024]{2,1,0:T(8,128)}, u32[]{:S(2)}, u32[]{:S(2)}) async-start(f32[16,51,1024]{2,1,0:T(8,128)} %reduce-scatter.2.cloned.1.call-done), calls=%async_computation.2 | async-start | bytes 7340032 | tf_op jit(solution)/shard_map/all_to_all | solution.py:199
  350.9 2.3 copy-start.5
  353.3 82.4 %copy-start.9 = (bf16[68,1024]{1,0:T(8,128)(2,1)}, bf16[68,1024]{1,0:T(8,128)(2,1)S(1)}, u32[]{:S(2)}) copy-start(bf16[68,1024]{1,0:T(8,128)(2,1)S(1)} %add_convert_fusion) | copy-start | bytes 417796
  436.0 1.5 copy-start.13
  437.5 6.0 %copy-start.1 = (bf16[2048,768]{1,0:T(8,128)(2,1)S(1)}, bf16[2048,768]{1,0:T(8,128)(2,1)}, u32[]{:S(2)}) copy-start(bf16[2048,768]{1,0:T(8,128)(2,1)} %param.28) | copy-start | bytes 9437188
Sparse Core Ops, SparseCore 0:
  29.3 32.7 all-reduce.2
  183.8 88.0 reduce-scatter.1
where the time goes:
time: 451 us; the launch traced here: 450 us
  waiting for transfers between devices  187 us (41%)
  blocking collectives  169 us (37%)
  matrix products  35.4 us (8%)
  local copies, waits for them, and re-layouts  27.4 us (6%)
  between operations  15.3 us (3%)
  other arithmetic  10 us (2%)
  starting transfers between devices  5.92 us (1%)
    reduce_scatter x1, waiting for transfers between devices, on_device(): summed = lax.psum_scatter(result, 'vp', scatter_dimension=2, tiled=True)  88.2 us
    all_to_all x1, blocking collectives, on_device(): lax.all_to_all(outgoing, 'ep', split_axis=0, concat_axis=0, tiled=True)  86.7 us
    all_gather x1, blocking collectives, on_device(): everyone = lax.all_gather(own_rows, ('ep', 'vp'), axis=0, tiled=True)  82.4 us
    all_to_all x1, waiting for transfers between devices, on_device(): lax.all_to_all(summed, 'ep', split_axis=0, concat_axis=0, tiled=True)  68.4 us
    psum x1, waiting for transfers between devices, on_device(): attn = lax.psum(partial_attn, 'vp')  30.6 us
    scatter x1, local copies, waits for them, and re-layouts, on_device(): outgoing = jnp.zeros((owners * capacity, model_width), jnp.bfloat16).at[t...  10.3 us
  transfers between devices with their start and end apart: 3, of which 3 were waited for; matrix products, arithmetic and copies ran while one was open for 0% of the time, Pallas kernels for 0%

commit v1 on v0

--- a/solution.py
+++ b/solution.py
@@ -1,6 +1,10 @@
+import functools
+
 import jax
 import jax.numpy as jnp
 from jax import lax
+from jax.experimental import pallas as pl
+from jax.experimental.pallas import tpu as pltpu
 from jax.sharding import PartitionSpec as P
 
 NOPE = 128
@@ -125,6 +129,414 @@
     return jnp.dot(
         head_out.reshape(row_count, head_count * VD), w_out, preferred_element_type=jnp.float32
     )
+
+
+MESH = pl.DeviceIdType.MESH
+SLAB = 80
+CODE_ROW = 72
+LANES = 128
+FINAL = 8
+
+
+def place():
+    e = lax.axis_index("ep")
+    return e // 4, (e // 2) % 2, e % 2, lax.axis_index("vp")
+
+
+def at(z, x, c, y):
+    return {"ep": z * 4 + x * 2 + c, "vp": y}
+
+
+def remote(src, dst, send, recv, target):
+    return pltpu.make_async_remote_copy(
+        src_ref=src, dst_ref=dst, send_sem=send, recv_sem=recv, device_id=target, device_id_type=MESH
+    )
+
+
+def gather_kernel(nz, part_ref, tok_ref, gain_ref, code_ref, resid_ref, all_ref, got, ys, yr, us, ur, ds, dr, xs, xr, cs, cr):
+    z, x, c, y = place()
+    barrier = pltpu.get_barrier_semaphore()
+    for target in (at(z, x, c, 1 - y), at(z, 1 - x, c, y), at(z, x, 1 - c, y)):
+        pl.semaphore_signal(barrier, inc=1, device_id=target, device_id_type=MESH)
+
+    for k in range(1, nz):
+        pl.semaphore_signal(barrier, inc=1, device_id=at((z + k) % nz, x, c, y), device_id_type=MESH)
+    pl.semaphore_wait(barrier, nz + 2)
+
+    swap = remote(part_ref, got, ys, yr, at(z, x, c, 1 - y))
+    swap.start()
+    swap.wait()
+    mine = z * 4 + x * 2 + c
+    attn = part_ref[...].astype(jnp.float32) + got[...].astype(jnp.float32)
+    resid = (tok_ref[...].astype(jnp.float32) + attn).astype(jnp.bfloat16)
+    resid_ref[...] = resid
+    ffn_in = rms_norm(resid.astype(jnp.float32), gain_ref[...])
+    all_ref[mine] = (ffn_in + code_ref[...].astype(jnp.float32)).astype(jnp.bfloat16)
+
+    def slab(zo, xo, co):
+        return all_ref.at[zo * 4 + xo * 2 + co]
+
+    def up(step):
+        s = slab(z - step, x, c)
+        return remote(s, s, us.at[step], ur.at[step], at(z + 1, x, c, y))
+
+    def up_in(step):
+        s = slab(z - 1 - step, x, c)
+        return remote(s, s, us.at[step], ur.at[step], at(z - 1, x, c, y))
+
+    def down(step):
+        s = slab(z + step, x, c)
+        return remote(s, s, ds.at[step], dr.at[step], at(z - 1, x, c, y))
+
+    def down_in(step):
+        s = slab(z + 1 + step, x, c)
+        return remote(s, s, ds.at[step], dr.at[step], at(z + 1, x, c, y))
+
+    def across(zo):
+        s = slab(zo, x, c)
+        return remote(s, s, xs.at[zo], xr.at[zo], at(z, 1 - x, c, y))
+
+    def across_in(zo):
+        s = slab(zo, 1 - x, c)
+        return remote(s, s, xs.at[zo], xr.at[zo], at(z, 1 - x, c, y))
+
+    def over(zo, xo):
+        s = slab(zo, xo, c)
+        return remote(s, s, cs.at[xo, zo], cr.at[xo, zo], at(z, x, 1 - c, y))
+
+    def over_in(zo, xo):
+        s = slab(zo, xo, 1 - c)
+        return remote(s, s, cs.at[xo, zo], cr.at[xo, zo], at(z, x, 1 - c, y))
+
+    def when(cond, fun):
+        pl.when(cond)(fun)
+
+    when(z + 1 < nz, lambda: up(0).start())
+    when(z > 0, lambda: down(0).start())
+    across(z).start()
+    over(z, x).start()
+    for step in range(nz - 1):
+
+        @pl.when(z - 1 - step >= 0)
+        def _():
+            up_in(step).wait_recv()
+            if step + 1 < nz - 1:
+                when(z + 1 < nz, lambda: up(step + 1).start())
+            across(z - 1 - step).start()
+            over(z - 1 - step, x).start()
+
+        @pl.when(z + 1 + step < nz)
+        def _():
+            down_in(step).wait_recv()
+            if step + 1 < nz - 1:
+                when(z > 0, lambda: down(step + 1).start())
+            across(z + 1 + step).start()
+            over(z + 1 + step, x).start()
+
+    def land(zo):
+        across_in(zo).wait_recv()
+        over(zo, 1 - x).start()
+
+    land(z)
+    for step in range(nz - 1):
+        when(z - 1 - step >= 0, lambda: land(z - 1 - step))
+        when(z + 1 + step < nz, lambda: land(z + 1 + step))
+    for zo in range(nz):
+        for xo in range(2):
+            over_in(zo, xo).wait_recv()
+    for zo in range(nz):
+        across(zo).wait_send()
+        for xo in range(2):
+            over(zo, xo).wait_send()
+    for step in range(nz - 1):
+        when((z + 1 < nz) & (z - step >= 0), lambda: up(step).wait_send())
+        when((z > 0) & (z + step < nz), lambda: down(step).wait_send())
+
+
+def gather(nz, partial, tokens, gain, code):
+    rows, width = tokens.shape
+    dma = pltpu.SemaphoreType.DMA
+    return pl.pallas_call(
+        functools.partial(gather_kernel, nz),
+        name="gather_tokens",
+        out_shape=(
+            jax.ShapeDtypeStruct((rows, width), jnp.bfloat16),
+            jax.ShapeDtypeStruct((nz * 4, rows, width), jnp.bfloat16),
+        ),
+        in_specs=[pl.BlockSpec(memory_space=pltpu.VMEM)] * 4,
+        out_specs=(pl.BlockSpec(memory_space=pltpu.VMEM),) * 2,
+        scratch_shapes=[
+            pltpu.VMEM((rows, width), jnp.bfloat16),
+            dma,
+            dma,
+            dma((nz - 1,)),
+            dma((nz - 1,)),
+            dma((nz - 1,)),
+            dma((nz - 1,)),
+            dma((nz,)),
+            dma((nz,)),
+            dma((2, nz)),
+            dma((2, nz)),
+        ],
+        compiler_params=pltpu.CompilerParams(
+            collective_id=0, has_side_effects=True, vmem_limit_bytes=40 * 1024 * 1024
+        ),
+    )(partial, tokens, gain, code)
+
+
+def reduce_kernel(nz, p_ref, resid_ref, out_ref, fin_ref, cin, s1, ya, xb, xa, yb, s2a, s2b, s3, zin, fbuf, c_s, c_r, ya_s, ya_r, xb_s, xb_r, xa_s, xa_r, yb_s, yb_r, z_s, z_r, f_s, f_r, g_s, g_r):
+    z, x, c, y = place()
+    share = s3.shape[-1]
+    half = share // 2
+    barrier = pltpu.get_barrier_semaphore()
+    plane = [(dx, dc, dy) for dx in range(2) for dc in range(2) for dy in range(2) if (dx, dc, dy) != (0, 0, 0)]
+
+    def beside(k):
+        dx, dc, dy = plane[k]
+        return at(z, (x + dx) % 2, (c + dc) % 2, (y + dy) % 2)
+
+    def along(k):
+        return at((z + k) % nz, x, c, y)
+
+    for k in range(len(plane)):
+        pl.semaphore_signal(barrier, inc=1, device_id=beside(k), device_id_type=MESH)
+    for k in range(1, nz):
+        pl.semaphore_signal(barrier, inc=1, device_id=along(k), device_id_type=MESH)
+    pl.semaphore_wait(barrier, len(plane) + nz - 1)
+
+    def add(a, b):
+        return (a.astype(jnp.float32) + b.astype(jnp.float32)).astype(jnp.bfloat16)
+
+    def cols(yo, part):
+        return pl.ds(pl.multiple_of(yo * share + part * half, LANES), half)
+
+    def core_copy(zo, xo):
+        return remote(
+            p_ref.at[zo * 4 + xo * 2 + 1 - c], cin.at[zo * 2 + xo], c_s.at[zo, xo], c_r.at[zo, xo], at(z, x, 1 - c, y)
+        )
+
+    def ya_copy(zo, xo):
+        return remote(
+            s1.at[zo * 2 + xo, :, cols(1 - y, 0)], ya.at[zo * 2 + xo], ya_s.at[zo, xo], ya_r.at[zo, xo], at(z, x, c, 1 - y)
+        )
+
+    def xb_copy(zo, yo):
+        return remote(
+            s1.at[zo * 2 + 1 - x, :, cols(yo, 1)], xb.at[zo * 2 + yo], xb_s.at[zo, yo], xb_r.at[zo, yo], at(z, 1 - x, c, y)
+        )
+
+    def xa_copy(zo):
+        return remote(s2a.at[zo * 2 + 1 - x], xa.at[zo], xa_s.at[zo], xa_r.at[zo], at(z, 1 - x, c, y))
+
+    def yb_copy(zo):
+        return remote(s2b.at[zo * 2 + 1 - y], yb.at[zo], yb_s.at[zo], yb_r.at[zo], at(z, x, c, 1 - y))
+
+    def z_copy(k):
+        return remote(s3.at[(z + k) % nz], zin.at[k - 1], z_s.at[k - 1], z_r.at[k - 1], along(k))
+
+    order = [(z + 1 + i) % nz for i in range(nz)]
+    for zo in order:
+        for xo in range(2):
+            core_copy(zo, xo).start()
+    for zo in order:
+        for xo in range(2):
+            core_copy(zo, xo).wait_recv()
+            s1[zo * 2 + xo] = add(p_ref[zo * 4 + xo * 2 + c], cin[zo * 2 + xo])
+            ya_copy(zo, xo).start()
+        for yo in range(2):
+            xb_copy(zo, yo).start()
+    for zo in order:
+        for side in range(2):
+            ya_copy(zo, side).wait_recv()
+            s2a[zo * 2 + side] = add(s1[zo * 2 + side, :, cols(y, 0)], ya[zo * 2 + side])
+            xb_copy(zo, side).wait_recv()
+            s2b[zo * 2 + side] = add(s1[zo * 2 + x, :, cols(side, 1)], xb[zo * 2 + side])
+        xa_copy(zo).start()
+        yb_copy(zo).start()
+    for i, zo in enumerate(order):
+        xa_copy(zo).wait_recv()
+        yb_copy(zo).wait_recv()
+        s3[zo, :, :half] = add(s2a[zo * 2 + x], xa[zo])
+        s3[zo, :, half:] = add(s2b[zo * 2 + y], yb[zo])
+        if i < nz - 1:
+            z_copy(i + 1).start()
+    total = s3[z].astype(jnp.float32)
+    for k in range(1, nz):
+        z_copy(k).wait_recv()
+        total = total + zin[k - 1].astype(jnp.float32)
+    own = resid_ref[:, pl.ds(pl.multiple_of(y * share, LANES), share)].astype(jnp.float32)
+    fbuf[...] = own + total
+    out_ref[...] = fbuf[...].astype(jnp.bfloat16)
+
+    def index(zo, xo, co, yo):
+        return (zo * 4 + xo * 2 + co) * 2 + yo
+
+    mine = index(z, x, c, y)
+    fin_ref[mine] = fbuf[63:71, :].astype(jnp.bfloat16)
+
+    def f_copy(k):
+        return remote(fin_ref.at[mine], fin_ref.at[mine], f_s.at[k - 1], f_r.at[k - 1], along(k))
+
+    def g_copy(k, d):
+        b = index((z + d) % nz, x, c, y)
+        return remote(fin_ref.at[b], fin_ref.at[b], g_s.at[k, d], g_r.at[k, d], beside(k))
+
+    def g_in(k, d):
+        dx, dc, dy = plane[k]
+        b = index((z + d) % nz, (x + dx) % 2, (c + dc) % 2, (y + dy) % 2)
+        return remote(fin_ref.at[b], fin_ref.at[b], g_s.at[k, d], g_r.at[k, d], beside(k))
+
+    def f_in(k):
+        b = index((z + nz - k) % nz, x, c, y)
+        return remote(fin_ref.at[b], fin_ref.at[b], f_s.at[k - 1], f_r.at[k - 1], along(k))
+
+    for k in range(1, nz):
+        f_copy(k).start()
+    for k in range(len(plane)):
+        g_copy(k, 0).start()
+    for d in range(1, nz):
+        f_in(d).wait_recv()
+        for k in range(len(plane)):
+            g_copy(k, nz - d).start()
+    for k in range(len(plane)):
+        for d in range(nz):
+            g_in(k, d).wait_recv()
+    for k in range(len(plane)):
+        for d in range(nz):
+            g_copy(k, d).wait_send()
+    for k in range(1, nz):
+        f_copy(k).wait_send()
+        z_copy(k).wait_send()
+    for zo in range(nz):
+        xa_copy(zo).wait_send()
+        yb_copy(zo).wait_send()
+        for side in range(2):
+            core_copy(zo, side).wait_send()
+            ya_copy(zo, side).wait_send()
+            xb_copy(zo, side).wait_send()
+
+
+def reduce_rows(nz, partial, resid):
+    owners, rows, width = partial.shape
+    share = width // 2
+    half = share // 2
+    dma = pltpu.SemaphoreType.DMA
+    buf = lambda *shape: pltpu.VMEM(shape, jnp.bfloat16)
+    return pl.pallas_call(
+        functools.partial(reduce_kernel, nz),
+        name="reduce_rows",
+        out_shape=(
+            jax.ShapeDtypeStruct((rows, share), jnp.bfloat16),
+            jax.ShapeDtypeStruct((owners * 2, FINAL, share), jnp.bfloat16),
+        ),
+        in_specs=[pl.BlockSpec(memory_space=pltpu.VMEM)] * 2,
+        out_specs=(pl.BlockSpec(memory_space=pltpu.VMEM),) * 2,
+        scratch_shapes=[
+            buf(nz * 2, rows, width),
+            buf(nz * 2, rows, width),
+            buf(nz * 2, rows, half),
+            buf(nz * 2, rows, half),
+            buf(nz, rows, half),
+            buf(nz, rows, half),
+            buf(nz * 2, rows, half),
+            buf(nz * 2, rows, half),
+            buf(nz, rows, share),
+            buf(nz - 1, rows, share),
+            pltpu.VMEM((rows, share), jnp.float32),
+        ]
+        + [dma((nz, 2))] * 6
+        + [dma((nz,))] * 4
+        + [dma((nz - 1,))] * 4
+        + [dma((7, nz))] * 2,
+        compiler_params=pltpu.CompilerParams(
+            collective_id=1, has_side_effects=True, vmem_limit_bytes=48 * 1024 * 1024
+        ),
+    )(partial, resid)
+
+
+def finish(final_rows, final_gain, head_weight):
+    final_normed = rms_norm(final_rows.astype(jnp.float32), final_gain).astype(jnp.bfloat16)
+    return jnp.dot(final_normed, head_weight, preferred_element_type=jnp.float32)
+
+
+def gate_code(expert_ids, expert_weights, owners, width):
+    named = expert_ids[:, :, None] == jnp.arange(owners, dtype=jnp.int32)
+    dense = jnp.sum(jnp.where(named, expert_weights[:, :, None], 0.0), axis=1)
+    flat = jnp.pad(dense.T, ((0, 0), (0, LANES - dense.shape[0]))).reshape(1, width)
+    high = lax.reduce_precision(flat, 8, 7)
+    middle = lax.reduce_precision(flat - high, 8, 7)
+    low = flat - high - middle
+    code = jnp.concatenate([high, middle, low], axis=0).astype(jnp.bfloat16)
+    return jnp.pad(code, ((CODE_ROW, SLAB - CODE_ROW - 3), (0, 0)))
+
+
+def on_block(
+    prefill_tokens,
+    decode_tokens,
+    request_order,
+    prefill_lengths,
+    decode_lengths,
+    latent_cache,
+    attn_gain,
+    w_query,
+    w_latent,
+    latent_gain,
+    key_up,
+    value_up,
+    w_out,
+    ffn_gain,
+    expert_ids,
+    expert_weights,
+    w_gate,
+    w_up,
+    w_down,
+    final_gain,
+    head_weight,
+):
+    owners = lax.axis_size("ep")
+    nz = owners // 4
+    partial_attn = attend(
+        prefill_tokens,
+        decode_tokens,
+        latent_cache,
+        prefill_lengths,
+        decode_lengths,
+        attn_gain,
+        w_query,
+        w_latent,
+        latent_gain,
+        key_up,
+        value_up,
+        w_out,
+    )
+    tokens = jnp.concatenate([prefill_tokens, decode_tokens], axis=0)
+    row_count, width = tokens.shape
+    blank = ((0, SLAB - row_count), (0, 0))
+    resid, arrived = gather(
+        nz,
+        jnp.pad(partial_attn.astype(jnp.bfloat16), blank),
+        jnp.pad(tokens, blank),
+        ffn_gain.reshape(1, width),
+        gate_code(expert_ids, expert_weights, owners, width),
+    )
+    me = lax.axis_index("ep")
+    codes = lax.dynamic_slice(arrived, (0, CODE_ROW, me * LANES), (owners, 3, LANES))
+    gates = jnp.sum(codes.astype(jnp.float32), axis=1)[:, :SLAB].reshape(owners * SLAB, 1)
+    flattened = arrived.reshape(owners * SLAB, width)
+    gated = jnp.dot(flattened, w_gate[0], preferred_element_type=jnp.float32)
+    upward = jnp.dot(flattened, w_up[0], preferred_element_type=jnp.float32)
+    hidden_act = (jax.nn.silu(gated) * upward).astype(jnp.bfloat16)
+    result = jnp.dot(hidden_act, w_down[0], preferred_element_type=jnp.float32) * gates
+    partial = result.astype(jnp.bfloat16).reshape(owners, SLAB, width)
+    share_rows, everyone = reduce_rows(nz, partial, resid)
+    layer_out = share_rows[:row_count]
+    decode_count = decode_tokens.shape[0]
+    everyone = everyone.reshape(owners, 2, FINAL, width // 2)[:, :, : 1 + decode_count]
+    everyone = jnp.transpose(everyone, (0, 2, 1, 3)).reshape(owners, 1 + decode_count, width)
+    prefill_last = everyone[:, 0]
+    decode_rows = everyone[:, 1:].reshape(owners * decode_count, width)[request_order]
+    final_rows = jnp.concatenate([prefill_last, decode_rows], axis=0)
+    return (layer_out, finish(final_rows, final_gain, head_weight))
 
 
 def on_device(
@@ -218,8 +630,9 @@
 
 
 def solution(mesh):
+    block = mesh.shape["vp"] == 2 and mesh.shape["ep"] == 16
     return jax.shard_map(
-        on_device,
+        on_block if block else on_device,
         mesh=mesh,
         in_specs=(
             P("ep", None),

time: 451 us -> 172 us (0.38)
  waiting for transfers between devices: 187 us -> 0 us
  blocking collectives: 169 us -> 0 us
  Pallas kernels: 0 us -> 95.4 us
  between operations: 15.3 us -> 1.72 us
  local copies, waits for them, and re-layouts: 27.4 us -> 19.1 us
  matrix products: 35.4 us -> 41.8 us
  starting transfers between devices: 5.92 us -> 0 us
    pallas_call x0 -> x2, Pallas kernels: none -> 95.4 us  [the longest x1 50 us: reduce_rows(): pl.pallas_call(functools.partial(reduce_kernel, nz), name='reduce_rows',...]
    reduce_scatter x1 -> x0, waiting for transfers between devices: 88.2 us -> none  [on_device(): summed = lax.psum_scatter(result, 'vp', scatter_dimension=2, tiled=True)]
    all_to_all x1 -> x0, blocking collectives: 86.7 us -> none  [on_device(): lax.all_to_all(outgoing, 'ep', split_axis=0, concat_axis=0, tiled=True)]
    all_gather x1 -> x0, blocking collectives: 82.4 us -> none  [on_device(): everyone = lax.all_gather(own_rows, ('ep', 'vp'), axis=0, tiled=True)]
    all_to_all x1 -> x0, waiting for transfers between devices: 68.4 us -> none  [on_device(): lax.all_to_all(summed, 'ep', split_axis=0, concat_axis=0, tiled=True)]
    psum x1 -> x0, waiting for transfers between devices: 30.6 us -> none  [on_device(): attn = lax.psum(partial_attn, 'vp')]
    scatter x1 -> x0, local copies, waits for them, and re-layouts: 10.3 us -> none  [on_device(): outgoing = jnp.zeros((owners * capacity, model_width), jnp.bfloat16).at[t...]
    reshape x7 -> x2, local copies, waits for them, and re-layouts: 9.42 us -> 2.22 us  [the longest x1 1.2 us: on_block(): jnp.transpose(everyone, (0, 2, 1, 3))]
  transfers between devices with their start and end apart: 3 -> 0, of which waited for: 3 -> 0; matrix products, arithmetic and copies ran while one was open for 0% -> 0% of each run, Pallas kernels for 0% -> 0%
where the time goes in v1:
time: 172 us; the launch traced here: 171 us
  Pallas kernels  95.4 us (55%)
  matrix products  41.8 us (24%)
  local copies, waits for them, and re-layouts  19.1 us (11%)
  other arithmetic  12.5 us (7%)
  between operations  1.72 us (1%)
    pallas_call x1, Pallas kernels, reduce_rows(): pl.pallas_call(functools.partial(reduce_kernel, nz), name='reduce_rows',...  50 us
    pallas_call x1, Pallas kernels, gather(): pl.pallas_call(functools.partial(gather_kernel, nz), name='gather_tokens'...  45.4 us
    dot_general x1, matrix products, on_block(): jnp.dot(hidden_act, w_down[0], preferred_element_type=jnp.float32) * gates  8.96 us
    dot_general x1, matrix products, finish(): jnp.dot(final_normed, head_weight, preferred_element_type=jnp.float32)  5.92 us
    dot_general x1, matrix products, on_block(): upward = jnp.dot(flattened, w_up[0], preferred_element_type=jnp.float32)  5.42 us
    unnamed x40, local copies, waits for them, and re-layouts  4.4 us
    dot_general x1, matrix products, on_block(): gated = jnp.dot(flattened, w_gate[0], preferred_element_type=jnp.float32)  3.92 us

profile of v1, /device:TPU:0, one launch (start us, length us, event | category | flops | bytes accessed | tf_op | source)
XLA Modules:
  0.0 170.5 jit_solution(12402515757982690035)
XLA Ops:
  0.7 1.1 constant_dynamic-update-slice_fusion.1
  2.7 2.5 %fusion.55 = f32[68,576]{1,0:T(8,128)S(1)} fusion(bf16[2048,576]{0,1:T(8,128)(2,1)} %param.29, bf16[68,2048]{1,0:T(8,128)(2,1)S(1)} %constant_dynamic-update-slice_fusion, f32[2048]{0:T(1024)} %param.27, f32[68]{0:T(128)S(1)} %add_rsqrt_fusion.2), kind=kOutput, calls=%fused_computation.73 | convolution fusion | flops 160989184 | bytes 2802960 | tf_op jit(solution)/shard_map/dot_general | solution.py:66
  6.8 1.4 fusion.57
  8.2 1.8 %reshape.292 = f32[68,4,192]{2,1,0:T(4,128)} reshape(f32[68,768]{1,0:T(8,128)} %fusion.57) | data formatting | bytes 417792 | tf_op jit(solution)/shard_map/reshape | solution.py:61
  10.1 1.1 subtract_convert_fusion
  12.3 2.2 %fusion.9 = bf16[68,4,512]{2,0,1:T(8,128)(2,1)} fusion(bf16[68,4,128]{2,1,0:T(4,128)(2,1)S(1)} %slice.145, bf16[512,512]{1,0:T(8,128)(2,1)} %param.31), kind=kOutput, calls=%fused_computation.16 | convolution fusion | flops 35790848 | bytes 872448 | tf_op jit(solution)/shard_map/rhn,lhn->rhl/dot_general | solution.py:72
  14.5 1.8 %pad_maximum_fusion.1 = bf16[68,4,576]{2,0,1:T(8,128)(2,1)} fusion(bf16[68,4,32]{2,0,1:T(8,128)(2,1)S(1)} %copy.76, bf16[68,4,32]{2,0,1:T(8,128)(2,1)S(1)} %copy.75, bf16[68,4,512]{2,0,1:T(8,128)(2,1)} %fusion.9), kind=kLoop, calls=%fused_computation.51 | loop fusion | flops 940032 | bytes 626688 | tf_op jit(solution)/shard_map/concatenate | solution.py:75
  20.4 1.7 slice.74
  22.1 1.9 %copy.88 = bf16[1,256,576]{2,1,0:T(8,128)(2,1)} copy(bf16[1,256,576]{1,2,0:T(8,128)(2,1)} %slice.74) | data formatting | bytes 589824
  24.0 2.2 %fusion.6 = f32[64,4,320]{2,0,1:T(8,128)} fusion(bf16[64,576]{1,0:T(8,128)(2,1)} %slice.99, bf16[256,576]{1,0:T(8,128)(2,1)} %bitcast.73, bf16[68,4,576]{2,0,1:T(8,128)(2,1)} %pad_maximum_fusion.1, pred[64,320]{1,0:T(8,128)(4,1)} %fusion.54), kind=kOutput, calls=%fused_computation.13 | convolution fusion | flops 95272960 | bytes 1089536 | tf_op jit(solution)/shard_map/chk,jk->chj/dot_general | solution.py:80
  26.2 2.3 %convolution_convert_fusion.2 = bf16[64,4,512]{2,0,1:T(8,128)(2,1)} fusion(bf16[256,576]{1,0:T(8,128)(2,1)} %bitcast.74, bf16[64,576]{1,0:T(8,128)(2,1)} %slice.99, f32[64,4,320]{2,0,1:T(8,128)} %fusion.6), kind=kOutput, calls=%fused_computation.10 | convolution fusion | flops 84836928 | bytes 1458176 | tf_op jit(solution)/shard_map/chj,jl->chl/dot_general | solution.py:97
  30.3 1.6 fusion.83
  32.6 1.6 fusion.20
  34.2 1.4 copy.80
  36.3 1.5 fusion.10
  38.0 2.1 %convolution_convert_fusion = bf16[68,2048]{1,0:T(8,128)(2,1)S(1)} fusion(bf16[68,512]{1,0:T(8,128)(2,1)S(1)} %bitcast.75, bf16[512,2048]{1,0:T(8,128)(2,1)} %param.33), kind=kOutput, calls=%fused_computation.8 | convolution fusion | flops 142745600 | bytes 2445312 | tf_op jit(solution)/shard_map/dot_general | solution.py:129
  40.3 45.4 %gather_tokens.1 = (bf16[80,2048]{1,0:T(8,128)(2,1)S(1)}, bf16[16,80,2048]{2,1,0:T(8,128)(2,1)S(1)}) custom-call(bf16[80,2048]{1,0:T(8,128)(2,1)S(1)} %pad.15.part_ref, bf16[80,2048]{1,0:T(8,128)(2,1)S(1)} %pad.16.tok_ref, f32[1,2048]{1,0:T(1,128)S(1)} %bitcast.69, bf16[80,2048]{1,0:T(8,128)(2,1)S(1)} %fusion.40.code_ref), custom_call_target="tpu_custom_call" | custom-call | tf_op jit(solution)/shard_map/gather_tokens/pallas_call | solution.py:259
  85.7 3.9 %fusion.3 = f32[1280,704]{0,1:T(8,128)S(1)} fusion(bf16[1280,2048]{1,0:T(8,128)(2,1)S(1)} %bitcast.70, bf16[1,2048,704]{1,2,0:T(8,128)(2,1)S(1)} %copy-done.14), kind=kOutput, calls=%fused_computation.6 | convolution fusion | flops 3690987520 | bytes 11730944 | tf_op jit(solution)/shard_map/dot_general | solution.py:526
  89.7 5.4 %fusion = bf16[1280,704]{0,1:T(8,128)(2,1)} fusion(bf16[1280,2048]{1,0:T(8,128)(2,1)S(1)} %bitcast.71, f32[1280,704]{0,1:T(8,128)S(1)} %fusion.3, bf16[1,2048,704]{1,2,0:T(8,128)(2,1)S(1)} %copy-done.15), kind=kOutput, calls=%fused_computation.3 | convolution fusion | flops 3696394240 | bytes 13533184 | tf_op jit(solution)/shard_map/dot_general | solution.py:527
  95.9 9.0 %multiply_convert_fusion = bf16[1280,2048]{1,0:T(8,128)(2,1)} fusion(bf16[1280,704]{0,1:T(8,128)(2,1)} %fusion, f32[1280]{0:T(1024)S(1)} %mul.211, bf16[1,704,2048]{2,1,0:T(8,128)(2,1)} %param.39), kind=kOutput, calls=%fused_computation.1 | convolution fusion | flops 3696230400 | bytes 9933824 | tf_op jit(solution)/shard_map/dot_general | solution.py:529
  104.9 50.0 %reduce_rows.1 = (bf16[80,1024]{1,0:T(8,128)(2,1)S(1)}, bf16[32,8,1024]{2,1,0:T(8,128)(2,1)S(1)}) custom-call(bf16[16,80,2048]{2,1,0:T(8,128)(2,1)} %bitcast.72, bf16[80,2048]{1,0:T(8,128)(2,1)S(1)} %get-tuple-element.7.resid_ref), custom_call_target="tpu_custom_call" | custom-call | tf_op jit(solution)/shard_map/reduce_rows/pallas_call | solution.py:425
  156.6 1.2 reshape.301
  160.5 1.4 gather_fusion
  163.9 5.9 %fusion.44 = f32[80,1600]{1,0:T(8,128)} fusion(bf16[2048,1600]{0,1:T(8,128)(2,1)} %param.41, f32[2048]{0:T(1024)S(1)} %copy-done.10, f32[80]{0:T(128)S(1)} %add_rsqrt_fusion, bf16[64,2048]{1,0:T(8,128)(2,1)} %gather_fusion, bf16[16,2048]{1,0:T(8,128)(2,1)S(1)} %slice_bitcast_fusion.1), kind=kOutput, calls=%fused_computation.56 | convolution fusion | flops 525434880 | bytes 7401792 | tf_op jit(solution)/shard_map/dot_general | solution.py:459
  (83 shorter events, 18.3 us)
Async XLA Ops:
  0.6 6.2 %copy-start = (bf16[2048,768]{1,0:T(8,128)(2,1)S(1)}, bf16[2048,768]{1,0:T(8,128)(2,1)}, u32[]{:S(2)}) copy-start(bf16[2048,768]{1,0:T(8,128)(2,1)} %param.28) | copy-start | bytes 9437188
  0.6 6.2 %copy-start.9 = (f32[2048]{0:T(1024)S(1)}, f32[2048]{0:T(1024)}, u32[]{:S(2)}) copy-start(f32[2048]{0:T(1024)} %param.27) | copy-start | bytes 24580
  0.7 5.3 %copy-start.16 = (s32[4]{0:T(128)S(1)}, s32[4]{0:T(128)}, u32[]{:S(2)}) copy-start(s32[4]{0:T(128)} %param.25) | copy-start | bytes 52
  5.2 0.8 copy-start.5
  6.8 10.5 %copy-start.13 = (f32[512]{0:T(512)S(1)}, f32[512]{0:T(512)}, u32[]{:S(2)}) copy-start(f32[512]{0:T(512)} %param.30) | copy-start | bytes 6148
  11.3 6.0 %copy-start.7 = (bf16[68,4,32]{2,0,1:T(8,128)(2,1)}, bf16[68,4,32]{2,0,1:T(8,128)(2,1)S(1)}, u32[]{:S(2)}) copy-start(bf16[68,4,32]{2,0,1:T(8,128)(2,1)S(1)} %copy.75) | copy-start | bytes 52228
  11.3 6.0 %copy-start.8 = (bf16[68,4,32]{2,0,1:T(8,128)(2,1)}, bf16[68,4,32]{2,0,1:T(8,128)(2,1)S(1)}, u32[]{:S(2)}) copy-start(bf16[68,4,32]{2,0,1:T(8,128)(2,1)S(1)} %copy.76) | copy-start | bytes 52228
  34.2 6.1 %copy-start.3 = (f32[2048]{0:T(1024)S(1)}, f32[2048]{0:T(1024)}, u32[]{:S(2)}) copy-start(f32[2048]{0:T(1024)} %param.34) | copy-start | bytes 24580
  35.5 4.5 %copy-start.11 = (f32[68,6]{0,1:T(8,128)S(1)}, f32[68,6]{0,1:T(8,128)}, u32[]{:S(2)}) copy-start(f32[68,6]{0,1:T(8,128)} %param.36) | copy-start | bytes 4900
  35.5 4.5 %copy-start.12 = (s32[68,6]{0,1:T(8,128)S(1)}, s32[68,6]{0,1:T(8,128)}, u32[]{:S(2)}) copy-start(s32[68,6]{0,1:T(8,128)} %param.35) | copy-start | bytes 4900
  36.3 49.4 %copy-start.14 = (bf16[1,2048,704]{1,2,0:T(8,128)(2,1)S(1)}, bf16[1,2048,704]{1,2,0:T(8,128)(2,1)}, u32[]{:S(2)}) copy-start(bf16[1,2048,704]{1,2,0:T(8,128)(2,1)} %param.37) | copy-start | bytes 8650756
  85.7 4.0 %copy-start.4 = (bf16[16,80,2048]{2,1,0:T(8,128)(2,1)}, bf16[16,80,2048]{2,1,0:T(8,128)(2,1)S(1)}, u32[]{:S(2)}) copy-start(bf16[16,80,2048]{2,1,0:T(8,128)(2,1)S(1)} %get-tuple-element.6) | copy-start | bytes 15728644
  85.7 3.9 %copy-start.15 = (bf16[1,2048,704]{1,2,0:T(8,128)(2,1)S(1)}, bf16[1,2048,704]{1,2,0:T(8,128)(2,1)}, u32[]{:S(2)}) copy-start(bf16[1,2048,704]{1,2,0:T(8,128)(2,1)} %param.38) | copy-start | bytes 8650756
  154.9 0.7 copy-start.1
  154.9 5.6 %copy-start.17 = (s32[64]{0:T(128)S(1)}, s32[64]{0:T(128)}, u32[]{:S(2)}) copy-start(s32[64]{0:T(128)} %param.23) | copy-start | bytes 772
  155.5 8.4 %copy-start.10 = (f32[2048]{0:T(1024)S(1)}, f32[2048]{0:T(1024)}, u32[]{:S(2)}) copy-start(f32[2048]{0:T(1024)} %param.40) | copy-start | bytes 24580
  157.8 0.7 copy-start.6
  163.9 5.9 %copy-start.2 = (bf16[80,1024]{1,0:T(8,128)(2,1)S(1)}, bf16[80,1024]{1,0:T(8,128)(2,1)}, u32[]{:S(2)}) copy-start(bf16[80,1024]{1,0:T(8,128)(2,1)} %copy-done.1) | copy-start | bytes 491524

commit v2 on v1

--- a/solution.py
+++ b/solution.py
@@ -284,7 +284,7 @@
     )(partial, tokens, gain, code)
 
 
-def reduce_kernel(nz, p_ref, resid_ref, out_ref, fin_ref, cin, s1, ya, xb, xa, yb, s2a, s2b, s3, zin, fbuf, c_s, c_r, ya_s, ya_r, xb_s, xb_r, xa_s, xa_r, yb_s, yb_r, z_s, z_r, f_s, f_r, g_s, g_r):
+def reduce_kernel(nz, p_ref, resid_ref, gain_ref, out_ref, normed_ref, fin_ref, cin, s1, ya, xb, xa, yb, s2a, s2b, s3, zin, fbuf, c_s, c_r, ya_s, ya_r, xb_s, xb_r, xa_s, xa_r, yb_s, yb_r, z_s, z_r, f_s, f_r, g_s, g_r):
     z, x, c, y = place()
     share = s3.shape[-1]
     half = share // 2
@@ -366,29 +366,30 @@
         total = total + zin[k - 1].astype(jnp.float32)
     own = resid_ref[:, pl.ds(pl.multiple_of(y * share, LANES), share)].astype(jnp.float32)
     fbuf[...] = own + total
-    out_ref[...] = fbuf[...].astype(jnp.bfloat16)
-
-    def index(zo, xo, co, yo):
-        return (zo * 4 + xo * 2 + co) * 2 + yo
-
-    mine = index(z, x, c, y)
-    fin_ref[mine] = fbuf[63:71, :].astype(jnp.bfloat16)
+    out_ref[...] = fbuf[: out_ref.shape[0], :].astype(jnp.bfloat16)
+
+    def piece(zo, xo, co, yo):
+        return fin_ref.at[zo * 4 + xo * 2 + co, :, pl.ds(pl.multiple_of(yo * share, LANES), share)]
+
+    mine = z * 4 + x * 2 + c
+    fin_ref[mine, :, pl.ds(pl.multiple_of(y * share, LANES), share)] = fbuf[63:71, :].astype(jnp.bfloat16)
 
     def f_copy(k):
-        return remote(fin_ref.at[mine], fin_ref.at[mine], f_s.at[k - 1], f_r.at[k - 1], along(k))
+        b = piece(z, x, c, y)
+        return remote(b, b, f_s.at[k - 1], f_r.at[k - 1], along(k))
 
     def g_copy(k, d):
-        b = index((z + d) % nz, x, c, y)
-        return remote(fin_ref.at[b], fin_ref.at[b], g_s.at[k, d], g_r.at[k, d], beside(k))
+        b = piece((z + d) % nz, x, c, y)
+        return remote(b, b, g_s.at[k, d], g_r.at[k, d], beside(k))
 
     def g_in(k, d):
         dx, dc, dy = plane[k]
-        b = index((z + d) % nz, (x + dx) % 2, (c + dc) % 2, (y + dy) % 2)
-        return remote(fin_ref.at[b], fin_ref.at[b], g_s.at[k, d], g_r.at[k, d], beside(k))
+        b = piece((z + d) % nz, (x + dx) % 2, (c + dc) % 2, (y + dy) % 2)
+        return remote(b, b, g_s.at[k, d], g_r.at[k, d], beside(k))
 
     def f_in(k):
-        b = index((z + nz - k) % nz, x, c, y)
-        return remote(fin_ref.at[b], fin_ref.at[b], f_s.at[k - 1], f_r.at[k - 1], along(k))
+        b = piece((z + nz - k) % nz, x, c, y)
+        return remote(b, b, f_s.at[k - 1], f_r.at[k - 1], along(k))
 
     for k in range(1, nz):
         f_copy(k).start()
@@ -401,6 +402,8 @@
     for k in range(len(plane)):
         for d in range(nz):
             g_in(k, d).wait_recv()
+    rows = rms_norm(fin_ref[...].astype(jnp.float32), gain_ref[...])
+    normed_ref[...] = rows.reshape(normed_ref.shape).astype(jnp.bfloat16)
     for k in range(len(plane)):
         for d in range(nz):
             g_copy(k, d).wait_send()
@@ -416,7 +419,7 @@
             xb_copy(zo, side).wait_send()
 
 
-def reduce_rows(nz, partial, resid):
+def reduce_rows(nz, partial, resid, gain, row_count):
     owners, rows, width = partial.shape
     share = width // 2
     half = share // 2
@@ -426,12 +429,13 @@
         functools.partial(reduce_kernel, nz),
         name="reduce_rows",
         out_shape=(
-            jax.ShapeDtypeStruct((rows, share), jnp.bfloat16),
-            jax.ShapeDtypeStruct((owners * 2, FINAL, share), jnp.bfloat16),
+            jax.ShapeDtypeStruct((row_count, share), jnp.bfloat16),
+            jax.ShapeDtypeStruct((owners * FINAL, width), jnp.bfloat16),
         ),
-        in_specs=[pl.BlockSpec(memory_space=pltpu.VMEM)] * 2,
+        in_specs=[pl.BlockSpec(memory_space=pltpu.VMEM)] * 3,
         out_specs=(pl.BlockSpec(memory_space=pltpu.VMEM),) * 2,
         scratch_shapes=[
+            buf(owners, FINAL, width),
             buf(nz * 2, rows, width),
             buf(nz * 2, rows, width),
             buf(nz * 2, rows, half),
@@ -451,12 +455,96 @@
         compiler_params=pltpu.CompilerParams(
             collective_id=1, has_side_effects=True, vmem_limit_bytes=48 * 1024 * 1024
         ),
-    )(partial, resid)
-
-
-def finish(final_rows, final_gain, head_weight):
-    final_normed = rms_norm(final_rows.astype(jnp.float32), final_gain).astype(jnp.bfloat16)
-    return jnp.dot(final_normed, head_weight, preferred_element_type=jnp.float32)
+    )(partial, resid, gain)
+
+
+def attention_kernel(heads, pf, rows_of, tok_ref, gain_ref, cos_ref, sin_ref, len_ref, lgain_ref, wq_hbm, wl_hbm, cache_hbm, ku_hbm, vu_hbm, wo_hbm, out_ref, wq, wl, cache, ku, vu, wo, sems):
+    pairs = [(wq_hbm, wq), (wl_hbm, wl), (cache_hbm, cache), (ku_hbm, ku), (vu_hbm, vu), (wo_hbm, wo)]
+    loads = [pltpu.make_async_copy(a, b, sems.at[i]) for i, (a, b) in enumerate(pairs)]
+    for load in loads:
+        load.start()
+    rows = tok_ref.shape[0]
+    f32, bf16 = jnp.float32, jnp.bfloat16
+    dot = functools.partial(jnp.dot, preferred_element_type=f32)
+    nt = lambda a, b: lax.dot_general(a, b, (((1,), (1,)), ((), ())), preferred_element_type=f32)
+    normed = rms_norm(tok_ref[...].astype(f32), gain_ref[...]).astype(bf16)
+    cosines, sines = cos_ref[...], sin_ref[...]
+
+    def turn(v):
+        half = ROPE // 2
+        return v * cosines + jnp.concatenate([v[:, half:], v[:, :half]], axis=1) * sines
+
+    loads[0].wait()
+    queries = dot(normed, wq[...])
+    loads[1].wait()
+    latent = dot(normed, wl[...])
+    key_lat = rms_norm(latent[:, :LAT], lgain_ref[...]).astype(bf16)
+    key_rope = turn(latent[:, LAT:]).astype(bf16)
+    loads[2].wait()
+    entries, cache_len = cache.shape[0], cache.shape[1]
+    old_lat = cache[:, :, :LAT].reshape(entries * cache_len, LAT)
+    old_rope = cache[:, :, LAT:].reshape(entries * cache_len, ROPE)
+    row = lax.broadcasted_iota(jnp.int32, (rows, 1), 0)
+    entry = jnp.where(row < pf, 0, jnp.where(row < rows_of, row - pf + 1, entries))
+    start = entry * cache_len
+    key = lax.broadcasted_iota(jnp.int32, (rows, entries * cache_len), 1)
+    old_seen = (key >= start) & (key < start + len_ref[...])
+    col = lax.broadcasted_iota(jnp.int32, (rows, rows), 1)
+    new_seen = (col == row) | ((row < pf) & (col <= row))
+    factor = 1.0 / jnp.sqrt(jnp.float32(NOPE + ROPE))
+    loads[3].wait()
+    outs = []
+    for h in range(heads):
+        base = h * (NOPE + ROPE)
+        q_nope = queries[:, base : base + NOPE].astype(bf16)
+        q_rope = turn(queries[:, base + NOPE : base + NOPE + ROPE]).astype(bf16)
+        absorbed = nt(q_nope, ku[:, h * NOPE : (h + 1) * NOPE]).astype(bf16)
+        old = (nt(absorbed, old_lat) + nt(q_rope, old_rope)) * factor
+        new = (nt(absorbed, key_lat) + nt(q_rope, key_rope)) * factor
+        old = jnp.exp(jnp.where(old_seen, old, -jnp.inf))
+        new = jnp.exp(jnp.where(new_seen, new, -jnp.inf))
+        total = jnp.sum(old, axis=1, keepdims=True) + jnp.sum(new, axis=1, keepdims=True)
+        old = (old / total).astype(bf16)
+        new = (new / total).astype(bf16)
+        context = (dot(old, old_lat) + dot(new, key_lat)).astype(bf16)
+        if h == 0:
+            loads[4].wait()
+        outs.append(dot(context, vu[:, h * VD : (h + 1) * VD]).astype(bf16))
+    loads[5].wait()
+    out_ref[...] = dot(jnp.concatenate(outs, axis=1), wo[...]).astype(bf16)
+
+
+def attention(tokens, pf, nd, prefill_len, decode_len, cached, attn_gain, w_query, w_latent, latent_gain, key_up, value_up, w_out):
+    rows, width = tokens.shape
+    spare = rows - pf - nd
+    steps = jnp.arange(pf, dtype=jnp.int32)
+    none = jnp.zeros((spare,), jnp.int32)
+    positions = jnp.concatenate([prefill_len[0] + steps, decode_len, none])
+    lengths = jnp.concatenate([prefill_len[0] + 0 * steps, decode_len, none])[:, None]
+    half = ROPE // 2
+    frequency = rope_base ** (-jnp.arange(half, dtype=jnp.float32) * 2.0 / ROPE)
+    angles = positions.astype(jnp.float32)[:, None] * frequency
+    cosines, sines = jnp.cos(angles), jnp.sin(angles)
+    vmem = pl.BlockSpec(memory_space=pltpu.VMEM)
+    hbm = pl.BlockSpec(memory_space=pl.ANY)
+    large = (w_query, w_latent, cached, key_up, value_up, w_out)
+    return pl.pallas_call(
+        functools.partial(attention_kernel, w_query.shape[1] // (NOPE + ROPE), pf, pf + nd),
+        name="attention",
+        out_shape=jax.ShapeDtypeStruct((rows, width), jnp.bfloat16),
+        in_specs=[vmem] * 6 + [hbm] * 6,
+        out_specs=vmem,
+        scratch_shapes=[pltpu.VMEM(a.shape, a.dtype) for a in large] + [pltpu.SemaphoreType.DMA((6,))],
+        compiler_params=pltpu.CompilerParams(vmem_limit_bytes=40 * 1024 * 1024),
+    )(
+        tokens,
+        attn_gain.reshape(1, width),
+        jnp.concatenate([cosines, cosines], axis=1),
+        jnp.concatenate([-sines, sines], axis=1),
+        lengths,
+        latent_gain.reshape(1, LAT),
+        *large,
+    )
 
 
 def gate_code(expert_ids, expert_weights, owners, width):
@@ -495,12 +583,17 @@
 ):
     owners = lax.axis_size("ep")
     nz = owners // 4
-    partial_attn = attend(
-        prefill_tokens,
-        decode_tokens,
-        latent_cache,
+    tokens = jnp.concatenate([prefill_tokens, decode_tokens], axis=0)
+    row_count, width = tokens.shape
+    prefill_count, decode_count = prefill_tokens.shape[0], decode_tokens.shape[0]
+    tokens = jnp.pad(tokens, ((0, SLAB - row_count), (0, 0)))
+    partial_attn = attention(
+        tokens,
+        prefill_count,
+        decode_count,
         prefill_lengths,
         decode_lengths,
+        latent_cache,
         attn_gain,
         w_query,
         w_latent,
@@ -509,13 +602,10 @@
         value_up,
         w_out,
     )
-    tokens = jnp.concatenate([prefill_tokens, decode_tokens], axis=0)
-    row_count, width = tokens.shape
-    blank = ((0, SLAB - row_count), (0, 0))
     resid, arrived = gather(
         nz,
-        jnp.pad(partial_attn.astype(jnp.bfloat16), blank),
-        jnp.pad(tokens, blank),
+        partial_attn,
+        tokens,
         ffn_gain.reshape(1, width),
         gate_code(expert_ids, expert_weights, owners, width),
     )
@@ -528,15 +618,17 @@
     hidden_act = (jax.nn.silu(gated) * upward).astype(jnp.bfloat16)
     result = jnp.dot(hidden_act, w_down[0], preferred_element_type=jnp.float32) * gates
     partial = result.astype(jnp.bfloat16).reshape(owners, SLAB, width)
-    share_rows, everyone = reduce_rows(nz, partial, resid)
-    layer_out = share_rows[:row_count]
-    decode_count = decode_tokens.shape[0]
-    everyone = everyone.reshape(owners, 2, FINAL, width // 2)[:, :, : 1 + decode_count]
-    everyone = jnp.transpose(everyone, (0, 2, 1, 3)).reshape(owners, 1 + decode_count, width)
-    prefill_last = everyone[:, 0]
-    decode_rows = everyone[:, 1:].reshape(owners * decode_count, width)[request_order]
-    final_rows = jnp.concatenate([prefill_last, decode_rows], axis=0)
-    return (layer_out, finish(final_rows, final_gain, head_weight))
+    layer_out, normed = reduce_rows(nz, partial, resid, final_gain.reshape(1, width), row_count)
+    slots = jnp.concatenate(
+        [
+            jnp.arange(owners, dtype=jnp.int32) * FINAL,
+            request_order // decode_count * FINAL + 1 + request_order % decode_count,
+        ]
+    )
+    chosen = (slots[:, None] == jnp.arange(owners * FINAL, dtype=jnp.int32)).astype(jnp.bfloat16)
+    final_normed = jnp.dot(chosen, normed, preferred_element_type=jnp.float32).astype(jnp.bfloat16)
+    logits = jnp.dot(final_normed, head_weight, preferred_element_type=jnp.float32)
+    return (layer_out, logits)
 
 
 def on_device(

time: 172 us -> 155 us (0.901)
  matrix products: 41.8 us -> 23 us
  Pallas kernels: 95.4 us -> 105 us
  other arithmetic: 12.5 us -> 4.92 us
    dot_general x11 -> x1, matrix products: 23.5 us -> 5.95 us  [on_block(): jnp.dot(final_normed, head_weight, preferred_element_type=jnp.float32)]
    unnamed x40 -> x43, local copies, waits for them, and re-layouts: 4.4 us -> 18.8 us
    pallas_call x0 -> x1, Pallas kernels: none -> 9.21 us  [attention(): pl.pallas_call(functools.partial(attention_kernel, w_query.shape[1] // (N...]
    slice x6 -> x0, local copies, waits for them, and re-layouts: 4.9 us -> none  [the longest x1 1.69 us: attend(): cached[0]]
    reshape x3 -> x0, local copies, waits for them, and re-layouts: 4.06 us -> none  [the longest x1 1.85 us: attend(): jnp.dot(normed, w_query, preferred_element_type=jnp.float32)]
    another operation x4 -> x1, other arithmetic: 2.97 us -> 0.02 us
    reduce_sum x3 -> x0, other arithmetic: 2.29 us -> none  [rms_norm(): jnp.mean(values * values, axis=-1, keepdims=True) + epsilon]
where the time goes in v2:
time: 155 us; the launch traced here: 154 us
  Pallas kernels  105 us (68%)
  matrix products  23 us (15%)
  local copies, waits for them, and re-layouts  19.5 us (13%)
  other arithmetic  4.92 us (3%)
  between operations  1.64 us (1%)
    pallas_call x1, Pallas kernels, reduce_rows(): pl.pallas_call(functools.partial(reduce_kernel, nz), name='reduce_rows',...  50.1 us
    pallas_call x1, Pallas kernels, gather(): pl.pallas_call(functools.partial(gather_kernel, nz), name='gather_tokens'...  45.4 us
    unnamed x43, local copies, waits for them, and re-layouts  18.8 us
    pallas_call x1, Pallas kernels, attention(): pl.pallas_call(functools.partial(attention_kernel, w_query.shape[1] // (N...  9.21 us
    dot_general x1, matrix products, on_block(): jnp.dot(hidden_act, w_down[0], preferred_element_type=jnp.float32) * gates  7.76 us
    dot_general x1, matrix products, on_block(): jnp.dot(final_normed, head_weight, preferred_element_type=jnp.float32)  5.95 us
    dot_general x1, matrix products, on_block(): upward = jnp.dot(flattened, w_up[0], preferred_element_type=jnp.float32)  5.4 us
    dot_general x1, matrix products, on_block(): gated = jnp.dot(flattened, w_gate[0], preferred_element_type=jnp.float32)  3.92 us

profile of v2, /device:TPU:0, one launch (start us, length us, event | category | flops | bytes accessed | tf_op | source)
XLA Modules:
  0.0 153.9 jit_solution(2402355319726100042)
XLA Ops:
  1.5 0.8 fusion.21
  2.5 0.7 pad_maximum_fusion
  3.2 0.7 select_reduce_fusion
  4.0 1.0 fusion.13
  5.0 0.7 copy.28.len_ref
  5.7 4.4 %copy.29.wl_hbm = bf16[2048,576]{1,0:T(8,128)(2,1)} copy(bf16[2048,576]{0,1:T(8,128)(2,1)} %param.29) | data formatting | bytes 4718592 | tf_op args[8]
  10.1 2.6 %copy.30.cache_hbm = bf16[5,256,576]{2,1,0:T(8,128)(2,1)} copy(bf16[5,256,576]{1,2,0:T(8,128)(2,1)} %param.26) | data formatting | bytes 2949120 | tf_op args[5]
  12.7 1.7 %copy-done.1 = bf16[2048,576]{1,0:T(8,128)(2,1)S(1)} copy-done((bf16[2048,576]{1,0:T(8,128)(2,1)S(1)}, bf16[2048,576]{1,0:T(8,128)(2,1)}, u32[]{:S(2)}) %copy-start.1) | copy-done | bytes 2359320
  14.5 1.4 copy-done.2
  15.9 1.9 %copy-done.3 = bf16[2048,768]{1,0:T(8,128)(2,1)S(1)} copy-done((bf16[2048,768]{1,0:T(8,128)(2,1)S(1)}, bf16[2048,768]{1,0:T(8,128)(2,1)}, u32[]{:S(2)}) %copy-start.3) | copy-done | bytes 3145752
  17.8 1.6 %copy-done.4 = bf16[512,2048]{1,0:T(8,128)(2,1)S(1)} copy-done((bf16[512,2048]{1,0:T(8,128)(2,1)S(1)}, bf16[512,2048]{1,0:T(8,128)(2,1)}, u32[]{:S(2)}) %copy-start.4) | copy-done | bytes 2097176
  19.4 1.0 copy-done.5
  20.4 1.0 copy-done.6
  21.5 0.8 copy-done.9
  22.2 0.8 copy-done.10
  23.0 0.8 copy-done.11
  23.8 9.2 %attention.1.part_ref = bf16[80,2048]{1,0:T(8,128)(2,1)S(1)} custom-call(bf16[80,2048]{1,0:T(8,128)(2,1)S(1)} %get-tuple-element.21.tok_ref, f32[1,2048]{1,0:T(1,128)S(1)} %bitcast.28, f32[80,64]{1,0:T(8,128)S(1)} %copy-done.9, f32[80,64]{1,0:T(8,128)S(1)} %copy-done.10, s32[80,1]{1,0:T(8,128)S(1)} %copy-done.11, f32[1,512]{1,0:T(1,128)S(1)} %bitcast.31, ...), custom_call_target="tpu_custom_call" | custom-call | tf_op jit(solution)/shard_map/attention/pallas_call | solution.py:531
  33.0 45.4 %gather_tokens.1 = (bf16[80,2048]{1,0:T(8,128)(2,1)S(1)}, bf16[16,80,2048]{2,1,0:T(8,128)(2,1)S(1)}) custom-call(bf16[80,2048]{1,0:T(8,128)(2,1)S(1)} %attention.1.part_ref, bf16[80,2048]{1,0:T(8,128)(2,1)S(1)} %get-tuple-element.21.tok_ref, f32[1,2048]{1,0:T(1,128)S(1)} %bitcast.29, bf16[80,2048]{1,0:T(8,128)(2,1)S(1)} %get-tuple-element.20.code_ref), custom_call_target="tpu_custom_call" | custom-call | tf_op jit(solution)/shard_map/gather_tokens/pallas_call | solution.py:259
  78.5 3.9 %fusion.3 = f32[1280,704]{0,1:T(8,128)S(1)} fusion(bf16[1280,2048]{1,0:T(8,128)(2,1)S(1)} %bitcast.32, bf16[1,2048,704]{1,2,0:T(8,128)(2,1)S(1)} %copy-done.17), kind=kOutput, calls=%fused_computation.5 | convolution fusion | flops 3690987520 | bytes 11730944 | tf_op jit(solution)/shard_map/dot_general | solution.py:616
  82.5 5.4 %fusion = bf16[1280,704]{0,1:T(8,128)(2,1)} fusion(bf16[1280,2048]{1,0:T(8,128)(2,1)S(1)} %bitcast.33, f32[1280,704]{0,1:T(8,128)S(1)} %fusion.3, bf16[1,2048,704]{1,2,0:T(8,128)(2,1)S(1)} %copy-done.18), kind=kOutput, calls=%fused_computation.2 | convolution fusion | flops 3696394240 | bytes 13533184 | tf_op jit(solution)/shard_map/dot_general | solution.py:617
  87.9 0.8 convert_reduce_fusion
  88.8 7.8 %multiply_convert_fusion = bf16[1280,2048]{1,0:T(8,128)(2,1)} fusion(bf16[1280,704]{0,1:T(8,128)(2,1)} %fusion, f32[1280]{0:T(1024)S(1)} %mul.51, bf16[1,704,2048]{2,1,0:T(8,128)(2,1)S(1)} %copy-done), kind=kOutput, calls=%fused_computation | convolution fusion | flops 3696230400 | bytes 9933824 | tf_op jit(solution)/shard_map/dot_general | solution.py:619
  96.5 50.1 %reduce_rows.1 = (bf16[68,1024]{1,0:T(8,128)(2,1)S(1)}, bf16[128,2048]{1,0:T(8,128)(2,1)S(1)}) custom-call(bf16[16,80,2048]{2,1,0:T(8,128)(2,1)} %bitcast.34, bf16[80,2048]{1,0:T(8,128)(2,1)S(1)} %copy-done.8, f32[1,2048]{1,0:T(1,128)S(1)} %bitcast.30), custom_call_target="tpu_custom_call" | custom-call | tf_op jit(solution)/shard_map/reduce_rows/pallas_call | solution.py:428
  147.2 5.9 %fusion.5 = f32[80,1600]{1,0:T(8,128)} fusion(bf16[2048,1600]{0,1:T(8,128)(2,1)} %param.41, bf16[128,2048]{1,0:T(8,128)(2,1)S(1)} %get-tuple-element.9, s32[80]{0:T(128)} %pad_add_fusion.2), kind=kOutput, calls=%fused_computation.8 | convolution fusion | flops 566405120 | bytes 7590208 | tf_op jit(solution)/shard_map/dot_general | solution.py:630
  (43 shorter events, 1.7 us)
Async XLA Ops:
  0.6 88.1 %copy-start = (bf16[1,704,2048]{2,1,0:T(8,128)(2,1)S(1)}, bf16[1,704,2048]{2,1,0:T(8,128)(2,1)}, u32[]{:S(2)}) copy-start(bf16[1,704,2048]{2,1,0:T(8,128)(2,1)} %param.39) | copy-start | bytes 8650756
  5.7 7.0 %copy-start.12 = (f32[2048]{0:T(1024)S(1)}, f32[2048]{0:T(1024)}, u32[]{:S(2)}) copy-start(f32[2048]{0:T(1024)} %param.27) | copy-start | bytes 24580
  5.7 7.0 %copy-start.15 = (f32[512]{0:T(512)S(1)}, f32[512]{0:T(512)}, u32[]{:S(2)}) copy-start(f32[512]{0:T(512)} %param.30) | copy-start | bytes 6148
  12.7 1.7 %copy-start.1 = (bf16[2048,576]{1,0:T(8,128)(2,1)S(1)}, bf16[2048,576]{1,0:T(8,128)(2,1)}, u32[]{:S(2)}) copy-start(bf16[2048,576]{1,0:T(8,128)(2,1)} %copy.29.wl_hbm) | copy-start | bytes 7077892
  14.5 1.4 copy-start.2
  15.9 1.9 %copy-start.3 = (bf16[2048,768]{1,0:T(8,128)(2,1)S(1)}, bf16[2048,768]{1,0:T(8,128)(2,1)}, u32[]{:S(2)}) copy-start(bf16[2048,768]{1,0:T(8,128)(2,1)} %wq_hbm.1) | copy-start | bytes 9437188
  17.8 1.6 %copy-start.4 = (bf16[512,2048]{1,0:T(8,128)(2,1)S(1)}, bf16[512,2048]{1,0:T(8,128)(2,1)}, u32[]{:S(2)}) copy-start(bf16[512,2048]{1,0:T(8,128)(2,1)} %wo_hbm.1) | copy-start | bytes 6291460
  19.4 1.0 copy-start.5
  20.4 1.0 copy-start.6
  21.5 0.8 copy-start.9
  22.2 0.8 copy-start.10
  23.0 0.8 copy-start.11
  23.8 9.2 %copy-start.13 = (f32[2048]{0:T(1024)S(1)}, f32[2048]{0:T(1024)}, u32[]{:S(2)}) copy-start(f32[2048]{0:T(1024)} %param.34) | copy-start | bytes 24580
  23.8 54.7 %copy-start.17 = (bf16[1,2048,704]{1,2,0:T(8,128)(2,1)S(1)}, bf16[1,2048,704]{1,2,0:T(8,128)(2,1)}, u32[]{:S(2)}) copy-start(bf16[1,2048,704]{1,2,0:T(8,128)(2,1)} %param.37) | copy-start | bytes 8650756
  78.5 4.0 %copy-start.7 = (bf16[80,2048]{1,0:T(8,128)(2,1)}, bf16[80,2048]{1,0:T(8,128)(2,1)S(1)}, u32[]{:S(2)}) copy-start(bf16[80,2048]{1,0:T(8,128)(2,1)S(1)} %get-tuple-element.7.resid_ref) | copy-start | bytes 983044
  78.5 4.0 %copy-start.16 = (bf16[16,80,2048]{2,1,0:T(8,128)(2,1)}, bf16[16,80,2048]{2,1,0:T(8,128)(2,1)S(1)}, u32[]{:S(2)}) copy-start(bf16[16,80,2048]{2,1,0:T(8,128)(2,1)S(1)} %get-tuple-element.6) | copy-start | bytes 15728644
  78.5 4.0 %copy-start.18 = (bf16[1,2048,704]{1,2,0:T(8,128)(2,1)S(1)}, bf16[1,2048,704]{1,2,0:T(8,128)(2,1)}, u32[]{:S(2)}) copy-start(bf16[1,2048,704]{1,2,0:T(8,128)(2,1)} %param.38) | copy-start | bytes 8650756
  88.7 7.8 %copy-start.8 = (bf16[80,2048]{1,0:T(8,128)(2,1)S(1)}, bf16[80,2048]{1,0:T(8,128)(2,1)}, u32[]{:S(2)}) copy-start(bf16[80,2048]{1,0:T(8,128)(2,1)} %copy-done.7) | copy-start | bytes 983044
  88.7 7.8 %copy-start.14 = (f32[2048]{0:T(1024)S(1)}, f32[2048]{0:T(1024)}, u32[]{:S(2)}) copy-start(f32[2048]{0:T(1024)} %param.40) | copy-start | bytes 24580
  96.5 50.1 %copy-start.19 = (s32[64]{0:T(128)S(1)}, s32[64]{0:T(128)}, u32[]{:S(2)}) copy-start(s32[64]{0:T(128)} %param.23) | copy-start | bytes 772

commit v3 on v2

--- a/solution.py
+++ b/solution.py
@@ -153,7 +153,7 @@
     )
 
 
-def gather_kernel(nz, part_ref, tok_ref, gain_ref, code_ref, resid_ref, all_ref, got, ys, yr, us, ur, ds, dr, xs, xr, cs, cr):
+def gather_kernel(nz, part_ref, tok_ref, gain_ref, code_ref, resid_ref, all_ref, got, ys, yr, us, ur, ds, dr, xs, xr, cs, cr, ws, wr, bs, br):
     z, x, c, y = place()
     barrier = pltpu.get_barrier_semaphore()
     for target in (at(z, x, c, 1 - y), at(z, 1 - x, c, y), at(z, x, 1 - c, y)):
@@ -173,8 +173,33 @@
     ffn_in = rms_norm(resid.astype(jnp.float32), gain_ref[...])
     all_ref[mine] = (ffn_in + code_ref[...].astype(jnp.float32)).astype(jnp.bfloat16)
 
+    width = tok_ref.shape[1]
+    band = width * 5 // 16 // LANES * LANES
+    main = width - band
+
     def slab(zo, xo, co):
-        return all_ref.at[zo * 4 + xo * 2 + co]
+        return all_ref.at[zo * 4 + xo * 2 + co, :, pl.ds(pl.multiple_of(y * band, LANES), main)]
+
+    def strip(zo, xo, co, yo):
+        return all_ref.at[zo * 4 + xo * 2 + co, :, pl.ds(pl.multiple_of(yo * main, LANES), band)]
+
+    def lend(zo, xo):
+        s = strip(zo, xo, c, y)
+        return remote(s, s, ws.at[xo, zo], wr.at[xo, zo], at(z, x, c, 1 - y))
+
+    def lend_in(zo, xo):
+        s = strip(zo, xo, c, 1 - y)
+        return remote(s, s, ws.at[xo, zo], wr.at[xo, zo], at(z, x, c, 1 - y))
+
+    def rest(zo, xo):
+        s = strip(zo, xo, c, 1 - y)
+        return remote(s, s, bs.at[xo, zo], br.at[xo, zo], at(z, x, 1 - c, y))
+
+    def rest_in(zo, xo):
+        s = strip(zo, xo, 1 - c, 1 - y)
+        return remote(s, s, bs.at[xo, zo], br.at[xo, zo], at(z, x, 1 - c, y))
+
+    others = [((z + k) % nz, (x + dx) % 2) for k in range(nz) for dx in range(2) if k + dx > 0]
 
     def up(step):
         s = slab(z - step, x, c)
@@ -215,6 +240,7 @@
     when(z > 0, lambda: down(0).start())
     across(z).start()
     over(z, x).start()
+    rest(z, x).start()
     for step in range(nz - 1):
 
         @pl.when(z - 1 - step >= 0)
@@ -223,6 +249,7 @@
             if step + 1 < nz - 1:
                 when(z + 1 < nz, lambda: up(step + 1).start())
             across(z - 1 - step).start()
+            lend(z - 1 - step, x).start()
             over(z - 1 - step, x).start()
 
         @pl.when(z + 1 + step < nz)
@@ -231,23 +258,32 @@
             if step + 1 < nz - 1:
                 when(z > 0, lambda: down(step + 1).start())
             across(z + 1 + step).start()
+            lend(z + 1 + step, x).start()
             over(z + 1 + step, x).start()
 
     def land(zo):
         across_in(zo).wait_recv()
+        lend(zo, 1 - x).start()
         over(zo, 1 - x).start()
 
     land(z)
     for step in range(nz - 1):
         when(z - 1 - step >= 0, lambda: land(z - 1 - step))
         when(z + 1 + step < nz, lambda: land(z + 1 + step))
+    for zo, xo in others:
+        lend_in(zo, xo).wait_recv()
+        rest(zo, xo).start()
     for zo in range(nz):
         for xo in range(2):
             over_in(zo, xo).wait_recv()
+            rest_in(zo, xo).wait_recv()
+    for zo, xo in others:
+        lend(zo, xo).wait_send()
     for zo in range(nz):
         across(zo).wait_send()
         for xo in range(2):
             over(zo, xo).wait_send()
+            rest(zo, xo).wait_send()
     for step in range(nz - 1):
         when((z + 1 < nz) & (z - step >= 0), lambda: up(step).wait_send())
         when((z > 0) & (z + step < nz), lambda: down(step).wait_send())
@@ -275,6 +311,10 @@
             dma((nz - 1,)),
             dma((nz,)),
             dma((nz,)),
+            dma((2, nz)),
+            dma((2, nz)),
+            dma((2, nz)),
+            dma((2, nz)),
             dma((2, nz)),
             dma((2, nz)),
         ],
@@ -477,13 +517,13 @@
     loads[0].wait()
     queries = dot(normed, wq[...])
     loads[1].wait()
-    latent = dot(normed, wl[...])
+    latent = nt(normed, wl[...])
     key_lat = rms_norm(latent[:, :LAT], lgain_ref[...]).astype(bf16)
     key_rope = turn(latent[:, LAT:]).astype(bf16)
     loads[2].wait()
-    entries, cache_len = cache.shape[0], cache.shape[1]
-    old_lat = cache[:, :, :LAT].reshape(entries * cache_len, LAT)
-    old_rope = cache[:, :, LAT:].reshape(entries * cache_len, ROPE)
+    entries, cache_len = cache.shape[0], cache.shape[2]
+    old_lat = [cache[e, :LAT, :] for e in range(entries)]
+    old_rope = [cache[e, LAT:, :] for e in range(entries)]
     row = lax.broadcasted_iota(jnp.int32, (rows, 1), 0)
     entry = jnp.where(row < pf, 0, jnp.where(row < rows_of, row - pf + 1, entries))
     start = entry * cache_len
@@ -499,14 +539,18 @@
         q_nope = queries[:, base : base + NOPE].astype(bf16)
         q_rope = turn(queries[:, base + NOPE : base + NOPE + ROPE]).astype(bf16)
         absorbed = nt(q_nope, ku[:, h * NOPE : (h + 1) * NOPE]).astype(bf16)
-        old = (nt(absorbed, old_lat) + nt(q_rope, old_rope)) * factor
+        old = [dot(absorbed, old_lat[e]) + dot(q_rope, old_rope[e]) for e in range(entries)]
+        old = jnp.concatenate(old, axis=1) * factor
         new = (nt(absorbed, key_lat) + nt(q_rope, key_rope)) * factor
         old = jnp.exp(jnp.where(old_seen, old, -jnp.inf))
         new = jnp.exp(jnp.where(new_seen, new, -jnp.inf))
         total = jnp.sum(old, axis=1, keepdims=True) + jnp.sum(new, axis=1, keepdims=True)
         old = (old / total).astype(bf16)
         new = (new / total).astype(bf16)
-        context = (dot(old, old_lat) + dot(new, key_lat)).astype(bf16)
+        context = dot(new, key_lat)
+        for e in range(entries):
+            context = context + nt(old[:, e * cache_len : (e + 1) * cache_len], old_lat[e])
+        context = context.astype(bf16)
         if h == 0:
             loads[4].wait()
         outs.append(dot(context, vu[:, h * VD : (h + 1) * VD]).astype(bf16))
@@ -526,8 +570,8 @@
     angles = positions.astype(jnp.float32)[:, None] * frequency
     cosines, sines = jnp.cos(angles), jnp.sin(angles)
     vmem = pl.BlockSpec(memory_space=pltpu.VMEM)
-    hbm = pl.BlockSpec(memory_space=pl.ANY)
-    large = (w_query, w_latent, cached, key_up, value_up, w_out)
+    hbm = pl.BlockSpec(memory_space=pltpu.HBM)
+    large = (w_query, w_latent.T, jnp.swapaxes(cached, 1, 2), key_up, value_up, w_out)
     return pl.pallas_call(
         functools.partial(attention_kernel, w_query.shape[1] // (NOPE + ROPE), pf, pf + nd),
         name="attention",
@@ -535,7 +579,7 @@
         in_specs=[vmem] * 6 + [hbm] * 6,
         out_specs=vmem,
         scratch_shapes=[pltpu.VMEM(a.shape, a.dtype) for a in large] + [pltpu.SemaphoreType.DMA((6,))],
-        compiler_params=pltpu.CompilerParams(vmem_limit_bytes=40 * 1024 * 1024),
+        compiler_params=pltpu.CompilerParams(vmem_limit_bytes=60 * 1024 * 1024),
     )(
         tokens,
         attn_gain.reshape(1, width),

time: 155 us -> 140 us (0.903)
  local copies, waits for them, and re-layouts: 19.5 us -> 2.47 us
  matrix products: 23 us -> 26.7 us
  Pallas kernels: 105 us -> 103 us
    unnamed x43 -> x21, local copies, waits for them, and re-layouts: 18.8 us -> 1.67 us
    dot_general x1, matrix products: 3.92 us -> 7.78 us  [on_block(): gated = jnp.dot(flattened, w_gate[0], preferred_element_type=jnp.float32)]
    pallas_call x1, Pallas kernels: 45.4 us -> 41.8 us  [gather(): pl.pallas_call(functools.partial(gather_kernel, nz), name='gather_tokens'...]
    pallas_call x1, Pallas kernels: 9.21 us -> 10.9 us  [attention(): pl.pallas_call(functools.partial(attention_kernel, w_query.shape[1] // (N...]
where the time goes in v3:
time: 140 us
  Pallas kernels  103 us (74%)
  matrix products  26.7 us (19%)
  other arithmetic  5.63 us (4%)
  local copies, waits for them, and re-layouts  2.47 us (2%)
  between operations  1.63 us (1%)
    pallas_call x1, Pallas kernels, reduce_rows(): pl.pallas_call(functools.partial(reduce_kernel, nz), name='reduce_rows',...  50.3 us
    pallas_call x1, Pallas kernels, gather(): pl.pallas_call(functools.partial(gather_kernel, nz), name='gather_tokens'...  41.8 us
    pallas_call x1, Pallas kernels, attention(): pl.pallas_call(functools.partial(attention_kernel, w_query.shape[1] // (N...  10.9 us
    dot_general x1, matrix products, on_block(): gated = jnp.dot(flattened, w_gate[0], preferred_element_type=jnp.float32)  7.78 us
    dot_general x1, matrix products, on_block(): jnp.dot(hidden_act, w_down[0], preferred_element_type=jnp.float32) * gates  7.63 us
    dot_general x1, matrix products, on_block(): jnp.dot(final_normed, head_weight, preferred_element_type=jnp.float32)  5.95 us
    dot_general x1, matrix products, on_block(): upward = jnp.dot(flattened, w_up[0], preferred_element_type=jnp.float32)  5.39 us

profile of v3, /device:TPU:0, one launch (start us, length us, event | category | flops | bytes accessed | tf_op | source)
XLA Modules:
  0.0 139.5 jit_solution(14765900466050801977)
XLA Ops:
  0.6 0.0 copy-start
  1.5 0.8 fusion.21
  2.3 0.2 fusion.17
  2.5 0.7 pad_maximum_fusion
  3.2 0.7 select_reduce_fusion
  4.0 1.8 %fusion.13 = (bf16[80,2048]{1,0:T(8,128)(2,1)S(1)}, bf16[80,2048]{1,0:T(8,128)(2,1)}) fusion(bf16[1,2048]{1,0:T(2,128)(2,1)S(1)} %get-tuple-element.11, bf16[1,2048]{1,0:T(2,128)(2,1)S(1)} %get-tuple-element.12, bf16[1,2048]{1,0:T(2,128)(2,1)S(1)} %get-tuple-element.10, bf16[4,2048]{1,0:T(4,128)(2,1)} %param.22, bf16[64,2048]{1,0:T(8,128)(2,1)} %param.21), kind=kLoop, calls=%fused_computation.19 | loop fusion | flops 3112960 | bytes 946176 | tf_op jit(solution)/shard_map/concatenate | solution.py:601
  5.7 0.7 copy.26.len_ref
  6.5 10.9 %attention.1.part_ref = bf16[80,2048]{1,0:T(8,128)(2,1)} custom-call(bf16[80,2048]{1,0:T(8,128)(2,1)} %get-tuple-element.21.tok_ref, f32[1,2048]{1,0:T(1,128)} %bitcast.40, f32[80,64]{1,0:T(8,128)} %get-tuple-element.18.cos_ref, f32[80,64]{1,0:T(8,128)} %get-tuple-element.19.sin_ref, s32[80,1]{1,0:T(8,128)} %copy.26.len_ref, f32[1,512]{1,0:T(1,128)} %bitcast.41, ...), custom_call_target="tpu_custom_call" | custom-call | tf_op jit(solution)/shard_map/attention/pallas_call | solution.py:575
  17.4 0.0 copy-done.1
  17.4 0.0 copy-done.5
  17.4 1.0 copy-done.2
  18.4 41.8 %gather_tokens.1 = (bf16[80,2048]{1,0:T(8,128)(2,1)S(1)}, bf16[16,80,2048]{2,1,0:T(8,128)(2,1)S(1)}) custom-call(bf16[80,2048]{1,0:T(8,128)(2,1)S(1)} %copy-done.2, bf16[80,2048]{1,0:T(8,128)(2,1)S(1)} %copy-done.1, f32[1,2048]{1,0:T(1,128)S(1)} %bitcast.30, bf16[80,2048]{1,0:T(8,128)(2,1)S(1)} %get-tuple-element.20.code_ref), custom_call_target="tpu_custom_call" | custom-call | tf_op jit(solution)/shard_map/gather_tokens/pallas_call | solution.py:295
  60.2 0.0 copy-start.3
  60.2 0.0 copy-start.8
  60.2 7.8 %fusion.3 = f32[1280,704]{0,1:T(8,128)S(1)} fusion(bf16[1280,2048]{1,0:T(8,128)(2,1)S(1)} %bitcast.32, bf16[1,2048,704]{1,2,0:T(8,128)(2,1)} %param.37), kind=kOutput, calls=%fused_computation.5 | convolution fusion | flops 3690987520 | bytes 11730944 | tf_op jit(solution)/shard_map/dot_general | solution.py:660
  68.1 5.4 %fusion = bf16[1280,704]{0,1:T(8,128)(2,1)} fusion(bf16[1280,2048]{1,0:T(8,128)(2,1)S(1)} %bitcast.33, f32[1280,704]{0,1:T(8,128)S(1)} %fusion.3, bf16[1,2048,704]{1,2,0:T(8,128)(2,1)S(1)} %copy-done.8), kind=kOutput, calls=%fused_computation.2 | convolution fusion | flops 3696394240 | bytes 13533184 | tf_op jit(solution)/shard_map/dot_general | solution.py:661
  73.4 0.8 convert_reduce_fusion
  74.2 0.1 mul.51
  74.3 0.0 copy-start.6
  74.3 7.6 %multiply_convert_fusion = bf16[1280,2048]{1,0:T(8,128)(2,1)} fusion(bf16[1280,704]{0,1:T(8,128)(2,1)} %fusion, f32[1280]{0:T(1024)S(1)} %mul.51, bf16[1,704,2048]{2,1,0:T(8,128)(2,1)S(1)} %copy-done), kind=kOutput, calls=%fused_computation | convolution fusion | flops 3696230400 | bytes 9933824 | tf_op jit(solution)/shard_map/dot_general | solution.py:663
  82.0 50.3 %reduce_rows.1 = (bf16[68,1024]{1,0:T(8,128)(2,1)S(1)}, bf16[128,2048]{1,0:T(8,128)(2,1)S(1)}) custom-call(bf16[16,80,2048]{2,1,0:T(8,128)(2,1)} %bitcast.34, bf16[80,2048]{1,0:T(8,128)(2,1)S(1)} %copy-done.4, f32[1,2048]{1,0:T(1,128)S(1)} %bitcast.31), custom_call_target="tpu_custom_call" | custom-call | tf_op jit(solution)/shard_map/reduce_rows/pallas_call | solution.py:468
  132.4 0.6 pad_add_fusion.2
  132.9 5.9 %fusion.5 = f32[80,1600]{1,0:T(8,128)} fusion(bf16[2048,1600]{0,1:T(8,128)(2,1)} %param.41, bf16[128,2048]{1,0:T(8,128)(2,1)S(1)} %get-tuple-element.9, s32[80]{0:T(128)} %pad_add_fusion.2), kind=kOutput, calls=%fused_computation.8 | convolution fusion | flops 566405120 | bytes 7590208 | tf_op jit(solution)/shard_map/dot_general | solution.py:674
  138.9 0.7 copy.29
  (21 shorter events, 0.1 us)
Async XLA Ops:
  0.6 73.7 %copy-start = (bf16[1,704,2048]{2,1,0:T(8,128)(2,1)S(1)}, bf16[1,704,2048]{2,1,0:T(8,128)(2,1)}, u32[]{:S(2)}) copy-start(bf16[1,704,2048]{2,1,0:T(8,128)(2,1)} %param.39) | copy-start | bytes 8650756
  6.5 10.9 %copy-start.1 = (bf16[80,2048]{1,0:T(8,128)(2,1)S(1)}, bf16[80,2048]{1,0:T(8,128)(2,1)}, u32[]{:S(2)}) copy-start(bf16[80,2048]{1,0:T(8,128)(2,1)} %get-tuple-element.21.tok_ref) | copy-start | bytes 983044
  6.5 10.9 %copy-start.5 = (f32[2048]{0:T(1024)S(1)}, f32[2048]{0:T(1024)}, u32[]{:S(2)}) copy-start(f32[2048]{0:T(1024)} %param.34) | copy-start | bytes 24580
  17.4 1.0 copy-start.2
  60.2 7.8 %copy-start.3 = (bf16[80,2048]{1,0:T(8,128)(2,1)}, bf16[80,2048]{1,0:T(8,128)(2,1)S(1)}, u32[]{:S(2)}) copy-start(bf16[80,2048]{1,0:T(8,128)(2,1)S(1)} %get-tuple-element.7.resid_ref) | copy-start | bytes 983044
  60.2 7.8 %copy-start.7 = (bf16[16,80,2048]{2,1,0:T(8,128)(2,1)}, bf16[16,80,2048]{2,1,0:T(8,128)(2,1)S(1)}, u32[]{:S(2)}) copy-start(bf16[16,80,2048]{2,1,0:T(8,128)(2,1)S(1)} %get-tuple-element.6) | copy-start | bytes 15728644
  60.2 7.8 %copy-start.8 = (bf16[1,2048,704]{1,2,0:T(8,128)(2,1)S(1)}, bf16[1,2048,704]{1,2,0:T(8,128)(2,1)}, u32[]{:S(2)}) copy-start(bf16[1,2048,704]{1,2,0:T(8,128)(2,1)} %param.38) | copy-start | bytes 8650756
  74.3 7.7 %copy-start.4 = (bf16[80,2048]{1,0:T(8,128)(2,1)S(1)}, bf16[80,2048]{1,0:T(8,128)(2,1)}, u32[]{:S(2)}) copy-start(bf16[80,2048]{1,0:T(8,128)(2,1)} %copy-done.3) | copy-start | bytes 983044
  74.3 7.6 %copy-start.6 = (f32[2048]{0:T(1024)S(1)}, f32[2048]{0:T(1024)}, u32[]{:S(2)}) copy-start(f32[2048]{0:T(1024)} %param.40) | copy-start | bytes 24580
  82.0 50.4 %copy-start.9 = (s32[64]{0:T(128)S(1)}, s32[64]{0:T(128)}, u32[]{:S(2)}) copy-start(s32[64]{0:T(128)} %param.23) | copy-start | bytes 772
